TPU v7x, 512 devices: a whole 4x8x8 slice. The times are simulated.
512 devices in a mesh: wide: 64 (over z, y_hi, core), narrow: 8 (over y_lo, x).
Axes of the slice: x: 4, y: 8 (y_hi: 4, y_lo: 2; y = y_hi * 2 + y_lo), z: 8, core: 2. Of those that a mesh axis runs over, the one named last changes fastest.
Arguments:
- tile_values: bfloat16 [3584, 512, 512], P(('wide', 'narrow')), may hold values from -0.25 to 0.25
- tile_row: int32 [3584], P(('wide', 'narrow')), may hold values from 0 to 1
- tile_col: int32 [3584], P(('wide', 'narrow')), may hold values from 0 to 7
- basis: float32 [524288, 256], P(('wide', 'narrow')), may hold values from -6 to 6
Outputs:
- next_basis: float32 [4096, 256], P('wide')
All inputs are finite; a program needn't handle non-finite values.
Results may differ from a plain program's by a relative error of at most 0.0032.
Values sent between devices are 32-bit elements; how exact they have to be, the bound alone decides.
No kernel may reach another device: no remote copies, remote signals or barrier semaphores. Data moves between devices by JAX's collectives and lax.ppermute only.
A program may use at most 64 MiB of HBM per device.

v0:
```python
import jax
import jax.numpy as jnp
from jax import lax
from jax.sharding import PartitionSpec as P

COLS_DEV = 64


def finish(owned_rows, gram_sum):
    factor = jnp.linalg.cholesky(gram_sum)
    return jax.scipy.linalg.solve_triangular(factor, owned_rows.T, lower=True).T


def gram_terms(owned_rows):
    return jnp.dot(
        owned_rows.T,
        owned_rows,
        precision=lax.Precision.HIGHEST,
        preferred_element_type=jnp.float32,
    )


def body(tile_values, tile_row, tile_col, basis):
    tile_edge = tile_values.shape[1]
    basis_width = basis.shape[1]
    blocks = basis.astype(jnp.bfloat16).reshape(basis.shape[0] // tile_edge, tile_edge, basis_width)
    chosen = jnp.take(blocks, tile_row, axis=0)
    products = jnp.einsum("tij,tik->tjk", tile_values, chosen, preferred_element_type=jnp.float32)
    col_blocks = COLS_DEV * lax.axis_size("wide") // tile_edge
    one_hot = (tile_col[None, :] == jnp.arange(col_blocks, dtype=jnp.int32)[:, None]).astype(
        jnp.float32
    )
    partial_value = jnp.einsum("ct,tjk->cjk", one_hot, products, precision=lax.Precision.HIGHEST)
    total_rows = col_blocks * tile_edge
    partial_value = partial_value.reshape(total_rows, basis_width)
    reduced = lax.psum_scatter(partial_value, "wide", scatter_dimension=0, tiled=True)
    owned_rows = lax.psum(reduced, "narrow")
    gram_sum = lax.psum(gram_terms(owned_rows), "wide") / total_rows
    return finish(owned_rows, gram_sum)


def solution(mesh):
    in_specs = (
        P(("wide", "narrow"), None, None),
        P(("wide", "narrow")),
        P(("wide", "narrow")),
        P(("wide", "narrow"), None),
    )
    out_specs = P("wide", None)
    return jax.shard_map(body, mesh=mesh, in_specs=in_specs, out_specs=out_specs, check_vma=False)
```

profile of v0, /device:TPU:1, one launch (start us, length us, event | category | flops | bytes accessed | tf_op | source)
XLA Modules:
  0.0 864.6 jit_solution(9576807460728252653)
XLA Ops:
  6.5 0.0 reduce-scatter.2.cloned.1.call-start
  6.5 0.7 compare_select_fusion
  7.2 0.7 compare_and_fusion
  7.9 1.3 convert_element_type.4
  9.2 0.7 gather_fusion
  9.8 5.1 fusion.2
  15.0 0.0 copy-start.1
  15.0 5.3 copy.10
  20.2 0.0 copy-done.1
  20.2 4.2 fusion
  24.5 3.2 copy.7
  27.7 0.0 reduce-scatter.2.cloned.1.call-update
  27.7 0.0 all-reduce.4.cloned.1.call-start
  27.7 157.9 %reduce-scatter.2.cloned.1.call-done = f32[64,256]{1,0:T(8,128)} async-done(((f32[4096,256]{1,0:T(8,128)}), f32[64,256]{1,0:T(8,128)}) %reduce-scatter.2.cloned.1.call-update) | async-done | bytes 65552 | tf_op jit(solution)/shard_map/reduce_scatter | solution.py:36
  185.6 0.0 all-reduce.4.cloned.1.call-update
  185.6 0.2 all-reduce.6.cloned.1.call-start
  185.9 83.3 %all-reduce.4.cloned.1.call-done = f32[64,256]{1,0:T(8,128)} async-done(((f32[64,256]{1,0:T(8,128)}), f32[64,256]{1,0:T(8,128)}) %all-reduce.4.cloned.1.call-update) | async-done | bytes 65552 | tf_op jit(solution)/shard_map/psum | solution.py:37
  269.2 0.0 copy-start
  269.2 2.1 fusion.19
  271.2 0.0 all-reduce.6.cloned.1.call-update
  271.3 523.6 %all-reduce.6.cloned.1.call-done = f32[256,256]{0,1:T(8,128)} async-done(((f32[256,256]{0,1:T(8,128)}), f32[256,256]{0,1:T(8,128)}) %all-reduce.6.cloned.1.call-update) | async-done | bytes 262160 | tf_op jit(solution)/shard_map/psum | solution.py:38
  794.8 1.0 broadcast_multiply_fusion
  795.8 0.1 copy.9
  796.0 1.0 fusion.6
  797.0 11.7 %cholesky.50 = f32[128,128]{1,0:T(8,128)S(1)} custom-call(f32[128,128]{1,0:T(8,128)S(1)} %cholesky.118), custom_call_target="Cholesky" | custom-call | tf_op jit(solution)/shard_map/jit(cholesky)/cholesky | solution.py:10
  808.7 9.8 %custom-call.15 = f32[1,128,128]{1,2,0:T(8,128)S(1)} custom-call(f32[1,128,128]{2,1,0:T(8,128)S(1)} %get-tuple-element.26), custom_call_target="InvertDiagBlocksLowerTriangular" | custom-call | tf_op jit(solution)/shard_map/jit(cholesky)/cholesky | solution.py:10
  818.5 0.2 constant_dynamic-update-slice_fusion.1
  818.8 0.3 convolution_subtract_fusion
  819.0 11.7 %cholesky.105 = f32[128,128]{1,0:T(8,128)S(1)} custom-call(f32[128,128]{1,0:T(8,128)S(1)} %convolution_subtract_fusion), custom_call_target="Cholesky" | custom-call | tf_op jit(solution)/shard_map/jit(cholesky)/cholesky | solution.py:10
  830.8 0.7 compare_reduce_fusion
  832.8 0.1 triangular_solve.57
  832.9 4.2 while.1
  833.1 0.7 fusion.28
  833.7 1.3 bitcast_dynamic-update-slice_fusion.2
  835.1 0.7 fusion.28
  835.8 1.3 bitcast_dynamic-update-slice_fusion.2
  837.1 19.7 %custom-call.16 = f32[2,128,128]{1,2,0:T(8,128)S(1)} custom-call(f32[2,128,128]{2,1,0:T(8,128)S(1)} %get-tuple-element.12), custom_call_target="InvertDiagBlocksLowerTriangular" | custom-call | tf_op jit(solution)/shard_map/jit(_solve_triangular)/triangular_solve | solution.py:11
  856.8 0.0 copy-done
  856.8 0.2 fusion.9
  857.0 0.2 convolution_subtract_fusion.1
  857.2 0.2 fusion.8
  857.4 0.6 maximum_bitcast_fusion
  (10 shorter events, 0.2 us)
Async XLA Ops:
  6.5 179.1 %reduce-scatter.2.cloned.1.call-start = ((), (), s32[]{:S(2)}) async-start(), calls=%async_computation.1 | async-start | bytes 4259840 | tf_op jit(solution)/shard_map/reduce_scatter | solution.py:36
  15.0 5.3 copy-start.1
  27.7 241.5 %all-reduce.4.cloned.1.call-start = ((), (), s32[]{:S(2)}) async-start(), calls=%async_computation.2 | async-start | bytes 131072 | tf_op jit(solution)/shard_map/psum | solution.py:37
  185.6 609.2 %all-reduce.6.cloned.1.call-start = ((), (), s32[]{:S(2)}) async-start(), calls=%async_computation.3 | async-start | bytes 524288 | tf_op jit(solution)/shard_map/psum | solution.py:38
  269.2 587.6 %copy-start = (f32[64,256]{1,0:T(8,128)S(1)}, f32[64,256]{1,0:T(8,128)}, u32[]{:S(2)}) copy-start(f32[64,256]{1,0:T(8,128)} %all-reduce.4.cloned.1.call-done) | copy-start | bytes 196612
Sparse Core Ops, SparseCore 0:
  27.8 157.7 reduce-scatter.1
  188.5 80.6 all-reduce.3
  272.1 522.7 all-reduce.5
where the time goes:
time: 865 us
  waiting for transfers between devices  765 us (88%)
  other arithmetic  58.9 us (7%)
  between operations  14.5 us (2%)
  local copies, waits for them, and re-layouts  13.4 us (2%)
  matrix products  12.5 us (1%)
    psum x1, waiting for transfers between devices, body(): gram_sum = lax.psum(gram_terms(owned_rows), 'wide') / total_rows  524 us
    reduce_scatter x1, waiting for transfers between devices, body(): lax.psum_scatter(partial_value, 'wide', scatter_dimension=0, tiled=True)  158 us
    psum x1, waiting for transfers between devices, body(): owned_rows = lax.psum(reduced, 'narrow')  83.3 us
    another operation x6, other arithmetic, finish(): factor = jnp.linalg.cholesky(gram_sum)  34 us
    another operation x3, other arithmetic, finish(): return jax.scipy.linalg.solve_triangular(factor, owned_rows.T, lower=True).T  19.7 us
  transfers between devices with their start and end apart: 3, of which 3 were waited for; matrix products, arithmetic and copies ran while one was open for 0% of the time, Pallas kernels for 0%

commit v1 on v0

v1 whole, which is shorter than its diff:
```python
import functools

import jax
import jax.numpy as jnp
from jax import lax
from jax.experimental import pallas as pl
from jax.experimental.pallas import tpu as pltpu
from jax.sharding import Mesh
from jax.sharding import PartitionSpec as P

AXES = ("z", "yh", "core", "yl", "x")
SIZES = (8, 4, 2, 2, 4)
TILE = 512
RANK = 256
COLS = 4096
HIGHEST = lax.Precision.HIGHEST
SUPER = 64


def product_kernel(row_ref, col_ref, core_ref, tile_ref, basis_ref, keep_ref, send_ref, rounded, total):
    step = pl.program_id(0)

    @pl.when(step == 0)
    def _():
        rounded[...] = basis_ref[...].astype(jnp.bfloat16).reshape(rounded.shape)
        total[...] = jnp.zeros_like(total)

    c = col_ref[step]
    res = lax.dot_general(
        tile_ref[0],
        rounded[row_ref[step]],
        (((0,), (0,)), ((), ())),
        preferred_element_type=jnp.float32,
    )
    for yh in range(4):
        for core in range(2):
            for yl in range(2):
                for x in range(4):
                    i = ((yh * 2 + core) * 2 + yl) * 4 + x
                    total[core, x, c, yh * 2 + yl] += res[8 * i : 8 * i + 8, :]

    @pl.when(step == pl.num_programs(0) - 1)
    def _():
        mine = core_ref[0]
        keep_ref[...] = total[mine]
        send_ref[...] = total[1 - mine]


def local_product(tile_values, tile_row, tile_col, basis, core):
    tiles = tile_values.shape[0]
    blocks = basis.shape[0] // TILE
    half = (4, 8, 8, 8, RANK)
    out = jax.ShapeDtypeStruct(half, jnp.float32)
    whole = pl.BlockSpec(half, lambda t, *_: (0, 0, 0, 0, 0))
    return pl.pallas_call(
        product_kernel,
        grid_spec=pltpu.PrefetchScalarGridSpec(
            num_scalar_prefetch=3,
            grid=(tiles,),
            in_specs=[
                pl.BlockSpec((1, TILE, TILE), lambda t, *_: (t, 0, 0)),
                pl.BlockSpec(basis.shape, lambda t, *_: (0, 0)),
            ],
            out_specs=[whole, whole],
            scratch_shapes=[
                pltpu.VMEM((blocks, TILE, RANK), jnp.bfloat16),
                pltpu.VMEM((2,) + half, jnp.float32),
            ],
        ),
        out_shape=[out, out],
        name="local_product",
    )(tile_row, tile_col, core, tile_values, basis)


def spread_kernel(parts_ref, out_ref):
    total = jnp.sum(parts_ref[...], axis=0)
    for i in range(out_ref.shape[0]):
        out_ref[i] = total


def sum_and_spread(parts, copies):
    return pl.pallas_call(
        spread_kernel,
        out_shape=jax.ShapeDtypeStruct((copies,) + parts.shape[1:], parts.dtype),
        name="sum_and_spread",
    )(parts)


def gram_kernel(rows_ref, out_ref):
    rows = rows_ref[...]
    gram = lax.dot_general(
        rows,
        rows,
        (((0,), (0,)), ((), ())),
        precision=HIGHEST,
        preferred_element_type=jnp.float32,
    )
    for i in range(RANK // 8):
        for h in range(2):
            out_ref[2 * i + h] = gram[8 * i : 8 * i + 8, 128 * h : 128 * h + 128]


def gram_terms(rows):
    return pl.pallas_call(
        gram_kernel,
        out_shape=jax.ShapeDtypeStruct((64, 8, 128), jnp.float32),
        name="gram_terms",
    )(rows)


def lane(v, j):
    return jnp.broadcast_to(v[:, j : j + 1], (8, 128))


def sub(v, i):
    return jnp.broadcast_to(v[i : i + 1, :], v.shape)


def invert_factor(block, at):
    e = {}
    for j in range(8):
        column = lane(block, at + j)
        for i in range(j, 8):
            e[i, j] = sub(column, i)
    inv = {}
    for j in range(8):
        p = e[j, j]
        r = lax.rsqrt(p)
        r = r * (1.5 - 0.5 * (p * r) * r)
        inv[j, j] = r
        for i in range(j + 1, 8):
            e[i, j] = e[i, j] * r
        for k in range(j + 1, 8):
            for i in range(k, 8):
                e[i, k] = e[i, k] - e[i, j] * e[k, j]
    for i in range(1, 8):
        for j in range(i):
            acc = e[i, j] * inv[j, j]
            for k in range(j + 1, i):
                acc = acc + e[i, k] * inv[k, j]
            inv[i, j] = -acc * inv[i, i]
    place = lax.broadcasted_iota(jnp.int32, (8, 128), 0)
    zero = jnp.zeros((8, 128), jnp.float32)
    lower, upper = [], []
    for j in range(8):
        down = zero
        for i in range(j, 8):
            down = jnp.where(place == i, inv[i, j], down)
        lower.append(down)
        across = zero
        for i in range(j + 1):
            across = jnp.where(place == i, inv[j, i], across)
        upper.append(across)
    return lower, upper


def combine(columns, rows):
    out = []
    for piece in rows:
        acc = columns[0] * sub(piece, 0)
        for j in range(1, 8):
            acc = acc + columns[j] * sub(piece, j)
        out.append(acc)
    return out


def finish_kernel(gram_ref, rows_ref, out_ref, s_ref, a_ref, u_ref, ua_ref, y_ref):
    for i in range(RANK // 8):
        for h in range(2):
            s_ref[8 * i : 8 * i + 8, 128 * h : 128 * h + 128] = gram_ref[2 * i + h] * (1.0 / COLS)
    rows = rows_ref[...]
    a_ref[...] = jnp.concatenate([rows, jnp.zeros_like(rows)], axis=0).T

    def group(g, carry):
        first = pl.multiple_of(g * SUPER, SUPER)
        u_ref[...] = s_ref[pl.ds(first, SUPER), :]
        ua_ref[...] = a_ref[pl.ds(first, SUPER), :]
        panels = SUPER // 8
        for k in range(panels):
            here = slice(8 * k, 8 * k + 8)
            pieces = [u_ref[here, 0:128], u_ref[here, 128:256], ua_ref[here, :]]
            lower, upper = invert_factor(pieces[0], 8 * k)
            scaled = combine(lower, pieces)
            u_ref[here, 0:128] = scaled[0]
            u_ref[here, 128:256] = scaled[1]
            ua_ref[here, :] = scaled[2]
            if k + 1 < panels:
                w = combine(upper, scaled)
                wide_rows = [[sub(piece, j) for j in range(8)] for piece in w]
                for q in range(k + 1, panels):
                    there = slice(8 * q, 8 * q + 8)
                    old = [u_ref[there, 0:128], u_ref[there, 128:256], ua_ref[there, :]]
                    ms = [lane(old[0], 8 * k + j) for j in range(8)]
                    new = []
                    for piece, wr in zip(old, wide_rows):
                        acc = piece
                        for j in range(8):
                            acc = acc - ms[j] * wr[j]
                        new.append(acc)
                    u_ref[there, 0:128] = new[0]
                    u_ref[there, 128:256] = new[1]
                    ua_ref[there, :] = new[2]
        u, ua = u_ref[...], ua_ref[...]
        y_ref[pl.ds(first, SUPER), :] = ua

        @pl.when(g + 1 < RANK // SUPER)
        def _():
            dims = (((0,), (0,)), ((), ()))
            left = u
            back = pltpu.roll(left, first, 1)
            s_new = s_ref[...] - lax.dot_general(back, u, dims, precision=HIGHEST, preferred_element_type=jnp.float32)
            s_ref[...] = pltpu.roll(s_new, RANK - SUPER, 1)
            a_ref[...] = a_ref[...] - lax.dot_general(back, ua, dims, precision=HIGHEST, preferred_element_type=jnp.float32)

        return carry

    lax.fori_loop(0, RANK // SUPER, group, 0)
    out_ref[...] = y_ref[...].T[0:64, :]


def finish(gram_tiles, rows):
    return pl.pallas_call(
        finish_kernel,
        out_shape=jax.ShapeDtypeStruct((64, RANK), jnp.float32),
        scratch_shapes=[
            pltpu.VMEM((RANK, RANK), jnp.float32),
            pltpu.VMEM((RANK, 128), jnp.float32),
            pltpu.VMEM((SUPER, RANK), jnp.float32),
            pltpu.VMEM((SUPER, 128), jnp.float32),
            pltpu.VMEM((RANK, 128), jnp.float32),
        ],
        name="finish",
    )(gram_tiles, rows)


def exchange(x, axes):
    return lax.all_to_all(x, axes, 0, 0, tiled=True)


def partner_pairs():
    size = 1
    for s in SIZES:
        size *= s
    return [(i, i ^ 8) for i in range(size)]


def body(tile_values, tile_row, tile_col, basis):
    core = lax.axis_index("core").astype(jnp.int32).reshape(1)
    keep, send = local_product(tile_values, tile_row, tile_col, basis, core)
    got = lax.ppermute(send, AXES, partner_pairs())
    both = keep + got
    over_x = jnp.sum(exchange(both, ("x",)), axis=0)
    over_zy = exchange(over_x.reshape(64, 8, RANK), ("z", "yh", "yl"))
    rows = exchange(sum_and_spread(over_zy, 8), ("yl", "x")).reshape(64, RANK)
    terms = exchange(gram_terms(rows), ("z", "yh", "core"))
    gram_tiles = exchange(sum_and_spread(terms, 64), ("z", "yh", "core"))
    return finish(gram_tiles, rows)


def solution(mesh):
    fine = Mesh(mesh.devices.reshape(SIZES), AXES)
    in_specs = (P(AXES, None, None), P(AXES), P(AXES), P(AXES, None))
    return jax.shard_map(
        body, mesh=fine, in_specs=in_specs, out_specs=P(("z", "yh", "core"), None), check_vma=False
    )
```

time: 865 us -> 156 us (0.18)
  waiting for transfers between devices: 765 us -> 3.97 us
  blocking collectives: 0 us -> 112 us
  other arithmetic: 58.9 us -> 2.13 us
  Pallas kernels: 0 us -> 28.6 us
  between operations: 14.5 us -> 0.03 us
  local copies, waits for them, and re-layouts: 13.4 us -> 0 us
  matrix products: 12.5 us -> 0 us
    psum x2 -> x0, waiting for transfers between devices: 607 us -> none  [the longest x1 524 us: body(): gram_sum = lax.psum(gram_terms(owned_rows), 'wide') / total_rows]
    reduce_scatter x1 -> x0, waiting for transfers between devices: 158 us -> none  [body(): lax.psum_scatter(partial_value, 'wide', scatter_dimension=0, tiled=True)]
    all_to_all x0 -> x5, blocking collectives: none -> 112 us  [exchange(): return lax.all_to_all(x, axes, 0, 0, tiled=True)]
    another operation x9 -> x0, other arithmetic: 53.7 us -> none  [the longest x6 34 us: finish(): factor = jnp.linalg.cholesky(gram_sum)]
    pallas_call x0 -> x5, Pallas kernels: none -> 28.6 us  [the longest x1 14 us: finish(): pl.pallas_call(finish_kernel, out_shape=jax.ShapeDtypeStruct((64, RANK),...]
    dot_general x3 -> x0, matrix products: 11.4 us -> none  [the longest x1 5.14 us: body(): jnp.einsum('tij,tik->tjk', tile_values, chosen, preferred_element_type=jn...]
    ppermute x0 -> x1, starting transfers between devices: none -> 8.73 us  [body(): got = lax.ppermute(send, AXES, partner_pairs())]
  transfers between devices with their start and end apart: 3 -> 1, of which waited for: 3 -> 1; matrix products, arithmetic and copies ran while one was open for 0% -> 0% of each run, Pallas kernels for 0% -> 0%
where the time goes in v1:
time: 156 us; the launch traced here: 155 us
  blocking collectives  112 us (72%)
  Pallas kernels  28.6 us (18%)
  starting transfers between devices  8.73 us (6%)
  waiting for transfers between devices  3.97 us (3%)
  other arithmetic  2.13 us (1%)
    all_to_all x5, blocking collectives, exchange(): return lax.all_to_all(x, axes, 0, 0, tiled=True)  112 us
    pallas_call x1, Pallas kernels, finish(): pl.pallas_call(finish_kernel, out_shape=jax.ShapeDtypeStruct((64, RANK),...  14 us
    pallas_call x1, Pallas kernels, local_product(): pl.pallas_call(product_kernel, grid_spec=pltpu.PrefetchScalarGridSpec(num...  9.17 us
    ppermute x1, starting transfers between devices, body(): got = lax.ppermute(send, AXES, partner_pairs())  8.73 us
    ppermute x1, waiting for transfers between devices, body(): got = lax.ppermute(send, AXES, partner_pairs())  3.97 us
    pallas_call x2, Pallas kernels, sum_and_spread(): pl.pallas_call(spread_kernel, out_shape=jax.ShapeDtypeStruct((copies,) +...  3.47 us
  transfers between devices with their start and end apart: 1, of which 1 were waited for; matrix products, arithmetic and copies ran while one was open for 0% of the time, Pallas kernels for 0%

profile of v1, /device:TPU:1, one launch (start us, length us, event | category | flops | bytes accessed | tf_op | source)
XLA Modules:
  0.0 155.4 jit_solution(7305034067467108281)
XLA Ops:
  0.0 9.2 %local_product.1 = (f32[4,8,8,8,256]{4,3,2,1,0:T(8,128)}, f32[4,8,8,8,256]{4,3,2,1,0:T(8,128)}) custom-call(s32[7]{0:T(128)} %row_ref.1, s32[7]{0:T(128)} %col_ref.1, s32[1]{0:T(128)} %bitcast.core_ref, bf16[7,512,512]{2,1,0:T(8,128)(2,1)} %tile_ref.1, f32[1024,256]{1,0:T(8,128)} %basis_ref.1), custom_call_target="tpu_custom_call" | custom-call | tf_op jit(solution)/shard_map/local_product/pallas_call | solution.py:55
  9.2 8.7 %collective-permute-start = (f32[4,8,8,8,256]{4,3,2,1,0:T(8,128)}, f32[4,8,8,8,256]{4,3,2,1,0:T(8,128)S(1)}, u32[]{:S(2)}, u32[]{:S(2)}) collective-permute-start(f32[4,8,8,8,256]{4,3,2,1,0:T(8,128)} %get-tuple-element.8), channel_id=1, source_target_pairs={{0,8},{1,9},{2,10},{3,11},{4,12},{5,13},{6,14},{7,15},{8,0},{9,1},... | collective-permute-start | bytes 6291464 | tf_op jit(solution)/shard_map/ppermute | solution.py:250
  17.9 4.0 %collective-permute-done = f32[4,8,8,8,256]{4,3,2,1,0:T(8,128)S(1)} collective-permute-done((f32[4,8,8,8,256]{4,3,2,1,0:T(8,128)}, f32[4,8,8,8,256]{4,3,2,1,0:T(8,128)S(1)}, u32[]{:S(2)}, u32[]{:S(2)}) %collective-permute-start) | collective-permute-done | bytes 2097184 | tf_op jit(solution)/shard_map/ppermute | solution.py:250
  21.9 2.0 %add.3 = f32[4,8,8,8,256]{4,3,2,1,0:T(8,128)S(1)} add(f32[4,8,8,8,256]{4,3,2,1,0:T(8,128)} %get-tuple-element.7, f32[4,8,8,8,256]{4,3,2,1,0:T(8,128)S(1)} %collective-permute-done) | non-fusion elementwise | flops 524288 | bytes 6291456 | tf_op jit(solution)/shard_map/add | solution.py:251
  23.8 28.5 %all_to_all.25 = f32[4,8,8,8,256]{4,3,2,1,0:T(8,128)S(1)} all-to-all(f32[4,8,8,8,256]{4,3,2,1,0:T(8,128)S(1)} %add.3), channel_id=1, replica_groups=mesh['z'=8,'yh'=4,'core'=2,'yl'=2,'x'=4] {'x'}, dimensions={0} | all-to-all | bytes 4194304 | tf_op jit(solution)/shard_map/all_to_all | solution.py:237
  52.4 0.2 reduce_sum.9
  52.6 27.3 %all_to_all.26.parts_ref = f32[64,8,256]{2,1,0:T(8,128)} all-to-all(f32[64,8,256]{2,1,0:T(8,128)S(1)} %bitcast.3), channel_id=1, replica_groups=mesh['z'=8,'yh'=4,'core'=2,'yl'=2,'x'=4] {'z','yh','yl'}, dimensions={0} | all-to-all | bytes 1048576 | tf_op jit(solution)/shard_map/all_to_all | solution.py:237
  79.8 1.7 %sum_and_spread.2 = f32[8,8,256]{2,1,0:T(8,128)} custom-call(f32[64,8,256]{2,1,0:T(8,128)} %all_to_all.26.parts_ref), custom_call_target="tpu_custom_call" | custom-call | tf_op jit(solution)/shard_map/sum_and_spread/pallas_call | solution.py:82
  81.6 9.2 %all_to_all.27 = f32[8,8,256]{2,1,0:T(8,128)} all-to-all(f32[8,8,256]{2,1,0:T(8,128)} %sum_and_spread.2), channel_id=1, replica_groups=mesh['z'=8,'yh'=4,'core'=2,'yl'=2,'x'=4] {'yl','x'}, dimensions={0} | all-to-all | bytes 131072 | tf_op jit(solution)/shard_map/all_to_all | solution.py:237
  90.8 2.0 %gram_terms.1 = f32[64,8,128]{2,1,0:T(8,128)} custom-call(f32[64,256]{1,0:T(8,128)} %bitcast.4), custom_call_target="tpu_custom_call" | custom-call | tf_op jit(solution)/shard_map/gram_terms/pallas_call | solution.py:104
  92.8 26.3 %all_to_all.28.parts_ref = f32[64,8,128]{2,1,0:T(8,128)} all-to-all(f32[64,8,128]{2,1,0:T(8,128)} %gram_terms.1), channel_id=1, replica_groups=mesh['z'=8,'yh'=4,'core'=2,'yl'=2,'x'=4] {'z','yh','core'}, dimensions={0} | all-to-all | bytes 524288 | tf_op jit(solution)/shard_map/all_to_all | solution.py:237
  119.1 1.7 %sum_and_spread.3 = f32[64,8,128]{2,1,0:T(8,128)} custom-call(f32[64,8,128]{2,1,0:T(8,128)} %all_to_all.28.parts_ref), custom_call_target="tpu_custom_call" | custom-call | tf_op jit(solution)/shard_map/sum_and_spread/pallas_call | solution.py:82
  120.8 20.5 %all_to_all.29.gram_ref = f32[64,8,128]{2,1,0:T(8,128)} all-to-all(f32[64,8,128]{2,1,0:T(8,128)} %sum_and_spread.3), channel_id=1, replica_groups=mesh['z'=8,'yh'=4,'core'=2,'yl'=2,'x'=4] {'z','yh','core'}, dimensions={0} | all-to-all | bytes 524288 | tf_op jit(solution)/shard_map/all_to_all | solution.py:237
  141.4 14.0 %finish.1 = f32[64,256]{1,0:T(8,128)} custom-call(f32[64,8,128]{2,1,0:T(8,128)} %all_to_all.29.gram_ref, f32[64,256]{1,0:T(8,128)} %bitcast.5), custom_call_target="tpu_custom_call" | custom-call | tf_op jit(solution)/shard_map/finish/pallas_call | solution.py:222
Async XLA Ops:
  9.2 12.7 %collective-permute-start = (f32[4,8,8,8,256]{4,3,2,1,0:T(8,128)}, f32[4,8,8,8,256]{4,3,2,1,0:T(8,128)S(1)}, u32[]{:S(2)}, u32[]{:S(2)}) collective-permute-start(f32[4,8,8,8,256]{4,3,2,1,0:T(8,128)} %get-tuple-element.8), channel_id=1, source_target_pairs={{0,8},{1,9},{2,10},{3,11},{4,12},{5,13},{6,14},{7,15},{8,0},{9,1},... | collective-permute-start | bytes 6291464 | tf_op jit(solution)/shard_map/ppermute | solution.py:250

commit v2 on v1

--- a/solution.py
+++ b/solution.py
@@ -1,5 +1,3 @@
-import functools
-
 import jax
 import jax.numpy as jnp
 from jax import lax
@@ -8,50 +6,68 @@
 from jax.sharding import Mesh
 from jax.sharding import PartitionSpec as P
 
-AXES = ("z", "yh", "core", "yl", "x")
-SIZES = (8, 4, 2, 2, 4)
+AXES = ("zh", "zl", "yh", "core", "yl", "xh", "xl")
+SIZES = (4, 2, 4, 2, 2, 2, 2)
+NEAR = ("zl", "yl", "xl")
+FAR = ("zh", "yh", "xh")
+WIDE = ("zh", "zl", "yh", "core")
+NARROW = ("yl", "xh", "xl")
 TILE = 512
 RANK = 256
 COLS = 4096
 HIGHEST = lax.Precision.HIGHEST
 SUPER = 64
-
-
-def product_kernel(row_ref, col_ref, core_ref, tile_ref, basis_ref, keep_ref, send_ref, rounded, total):
+HALF = (8, 32, 8, RANK)
+IN_VMEM = pl.BlockSpec(memory_space=pltpu.VMEM)
+
+
+def held(x):
+    return pltpu.with_memory_space_constraint(x, pltpu.VMEM)
+
+
+def left_out(x):
+    return pltpu.with_memory_space_constraint(x, pltpu.HBM)
+
+
+def product_kernel(row_ref, col_ref, core_ref, tile_ref, basis_ref, keep_ref, send_ref, rounded):
     step = pl.program_id(0)
 
     @pl.when(step == 0)
     def _():
         rounded[...] = basis_ref[...].astype(jnp.bfloat16).reshape(rounded.shape)
-        total[...] = jnp.zeros_like(total)
+        keep_ref[...] = jnp.zeros_like(keep_ref)
+        send_ref[...] = jnp.zeros_like(send_ref)
 
     c = col_ref[step]
+    near, far = (c % 2) * 4, (c // 2) * 8
     res = lax.dot_general(
         tile_ref[0],
         rounded[row_ref[step]],
         (((0,), (0,)), ((), ())),
         preferred_element_type=jnp.float32,
     )
-    for yh in range(4):
-        for core in range(2):
-            for yl in range(2):
-                for x in range(4):
-                    i = ((yh * 2 + core) * 2 + yl) * 4 + x
-                    total[core, x, c, yh * 2 + yl] += res[8 * i : 8 * i + 8, :]
-
-    @pl.when(step == pl.num_programs(0) - 1)
+
+    def add(halves):
+        for yh in range(4):
+            for core in range(2):
+                for yl in range(2):
+                    for xh in range(2):
+                        for xl in range(2):
+                            i = (((yh * 2 + core) * 2 + yl) * 2 + xh) * 2 + xl
+                            halves[core][near + yl * 2 + xl, far + yh * 2 + xh] += res[8 * i : 8 * i + 8, :]
+
+    @pl.when(core_ref[0] == 0)
     def _():
-        mine = core_ref[0]
-        keep_ref[...] = total[mine]
-        send_ref[...] = total[1 - mine]
+        add((keep_ref, send_ref))
+
+    @pl.when(core_ref[0] == 1)
+    def _():
+        add((send_ref, keep_ref))
 
 
 def local_product(tile_values, tile_row, tile_col, basis, core):
     tiles = tile_values.shape[0]
     blocks = basis.shape[0] // TILE
-    half = (4, 8, 8, 8, RANK)
-    out = jax.ShapeDtypeStruct(half, jnp.float32)
-    whole = pl.BlockSpec(half, lambda t, *_: (0, 0, 0, 0, 0))
     return pl.pallas_call(
         product_kernel,
         grid_spec=pltpu.PrefetchScalarGridSpec(
@@ -61,29 +77,18 @@
                 pl.BlockSpec((1, TILE, TILE), lambda t, *_: (t, 0, 0)),
                 pl.BlockSpec(basis.shape, lambda t, *_: (0, 0)),
             ],
-            out_specs=[whole, whole],
-            scratch_shapes=[
-                pltpu.VMEM((blocks, TILE, RANK), jnp.bfloat16),
-                pltpu.VMEM((2,) + half, jnp.float32),
-            ],
+            out_specs=[IN_VMEM, IN_VMEM],
+            scratch_shapes=[pltpu.VMEM((blocks, TILE, RANK), jnp.bfloat16)],
         ),
-        out_shape=[out, out],
+        out_shape=[pltpu.VMEM(HALF, jnp.float32)] * 2,
+        compiler_params=pltpu.CompilerParams(vmem_limit_bytes=16 << 20),
         name="local_product",
-    )(tile_row, tile_col, core, tile_values, basis)
-
-
-def spread_kernel(parts_ref, out_ref):
-    total = jnp.sum(parts_ref[...], axis=0)
-    for i in range(out_ref.shape[0]):
-        out_ref[i] = total
+    )(left_out(tile_row), left_out(tile_col), core, left_out(tile_values), left_out(basis))
 
 
 def sum_and_spread(parts, copies):
-    return pl.pallas_call(
-        spread_kernel,
-        out_shape=jax.ShapeDtypeStruct((copies,) + parts.shape[1:], parts.dtype),
-        name="sum_and_spread",
-    )(parts)
+    total = jnp.sum(parts, axis=0)
+    return jnp.broadcast_to(total, (copies,) + total.shape)
 
 
 def gram_kernel(rows_ref, out_ref):
@@ -103,9 +108,12 @@
 def gram_terms(rows):
     return pl.pallas_call(
         gram_kernel,
-        out_shape=jax.ShapeDtypeStruct((64, 8, 128), jnp.float32),
+        in_specs=[IN_VMEM],
+        out_specs=IN_VMEM,
+        out_shape=pltpu.VMEM((64, 8, 128), jnp.float32),
+        compiler_params=pltpu.CompilerParams(vmem_limit_bytes=8 << 20),
         name="gram_terms",
-    )(rows)
+    )(held(rows))
 
 
 def lane(v, j):
@@ -221,6 +229,7 @@
 def finish(gram_tiles, rows):
     return pl.pallas_call(
         finish_kernel,
+        in_specs=[IN_VMEM, IN_VMEM],
         out_shape=jax.ShapeDtypeStruct((64, RANK), jnp.float32),
         scratch_shapes=[
             pltpu.VMEM((RANK, RANK), jnp.float32),
@@ -229,8 +238,9 @@
             pltpu.VMEM((SUPER, 128), jnp.float32),
             pltpu.VMEM((RANK, 128), jnp.float32),
         ],
+        compiler_params=pltpu.CompilerParams(vmem_limit_bytes=8 << 20),
         name="finish",
-    )(gram_tiles, rows)
+    )(held(gram_tiles), held(rows))
 
 
 def exchange(x, axes):
@@ -238,22 +248,17 @@
 
 
 def partner_pairs():
-    size = 1
-    for s in SIZES:
-        size *= s
-    return [(i, i ^ 8) for i in range(size)]
+    return [(i, i ^ 8) for i in range(512)]
 
 
 def body(tile_values, tile_row, tile_col, basis):
     core = lax.axis_index("core").astype(jnp.int32).reshape(1)
     keep, send = local_product(tile_values, tile_row, tile_col, basis, core)
-    got = lax.ppermute(send, AXES, partner_pairs())
-    both = keep + got
-    over_x = jnp.sum(exchange(both, ("x",)), axis=0)
-    over_zy = exchange(over_x.reshape(64, 8, RANK), ("z", "yh", "yl"))
-    rows = exchange(sum_and_spread(over_zy, 8), ("yl", "x")).reshape(64, RANK)
-    terms = exchange(gram_terms(rows), ("z", "yh", "core"))
-    gram_tiles = exchange(sum_and_spread(terms, 64), ("z", "yh", "core"))
+    both = keep + lax.ppermute(send, AXES, partner_pairs())
+    over_near = jnp.sum(exchange(both, NEAR), axis=0)
+    rows = exchange(sum_and_spread(exchange(over_near, FAR), 8), NARROW).reshape(64, RANK)
+    terms = exchange(gram_terms(rows), WIDE)
+    gram_tiles = exchange(sum_and_spread(terms, 64), WIDE)
     return finish(gram_tiles, rows)
 
 
@@ -261,5 +266,5 @@
     fine = Mesh(mesh.devices.reshape(SIZES), AXES)
     in_specs = (P(AXES, None, None), P(AXES), P(AXES), P(AXES, None))
     return jax.shard_map(
-        body, mesh=fine, in_specs=in_specs, out_specs=P(("z", "yh", "core"), None), check_vma=False
+        body, mesh=fine, in_specs=in_specs, out_specs=P(WIDE, None), check_vma=False
     )

time: 156 us -> 141 us (0.904)
  Pallas kernels: 28.6 us -> 20.6 us
  blocking collectives: 112 us -> 107 us
  other arithmetic: 2.13 us -> 0.52 us
    pallas_call x4 -> x2, Pallas kernels: 19.4 us -> 13.4 us  [the longest x1 13 us: finish(): pl.pallas_call(finish_kernel, in_specs=[IN_VMEM, IN_VMEM], out_shape=jax....]
    all_to_all x5, blocking collectives: 112 us -> 107 us  [exchange(): return lax.all_to_all(x, axes, 0, 0, tiled=True)]
    pallas_call x1, Pallas kernels: 9.17 us -> 7.18 us  [local_product(): pl.pallas_call(product_kernel, grid_spec=pltpu.PrefetchScalarGridSpec(num...]
    add x1, other arithmetic: 1.95 us -> 0.27 us  [body(): both = keep + lax.ppermute(send, AXES, partner_pairs())]
where the time goes in v2:
time: 141 us
  blocking collectives  107 us (76%)
  Pallas kernels  20.6 us (15%)
  starting transfers between devices  8.75 us (6%)
  waiting for transfers between devices  3.76 us (3%)
    all_to_all x5, blocking collectives, exchange(): return lax.all_to_all(x, axes, 0, 0, tiled=True)  107 us
    pallas_call x1, Pallas kernels, finish(): pl.pallas_call(finish_kernel, in_specs=[IN_VMEM, IN_VMEM], out_shape=jax....  13 us
    ppermute x1, starting transfers between devices, body(): both = keep + lax.ppermute(send, AXES, partner_pairs())  8.75 us
    pallas_call x1, Pallas kernels, local_product(): pl.pallas_call(product_kernel, grid_spec=pltpu.PrefetchScalarGridSpec(num...  7.18 us
    ppermute x1, waiting for transfers between devices, body(): both = keep + lax.ppermute(send, AXES, partner_pairs())  3.76 us
  transfers between devices with their start and end apart: 1, of which 1 were waited for; matrix products, arithmetic and copies ran while one was open for 0% of the time, Pallas kernels for 0%

profile of v2, /device:TPU:1, one launch (start us, length us, event | category | flops | bytes accessed | tf_op | source)
XLA Modules:
  0.0 140.7 jit_solution(9894248300807205327)
XLA Ops:
  0.0 7.2 %local_product.1 = (f32[8,32,8,256]{3,2,1,0:T(8,128)S(1)}, f32[8,32,8,256]{3,2,1,0:T(8,128)S(1)}) custom-call(s32[7]{0:T(128)} %row_ref.1, s32[7]{0:T(128)} %col_ref.1, s32[1]{0:T(128)} %bitcast.core_ref, bf16[7,512,512]{2,1,0:T(8,128)(2,1)} %tile_ref.1, f32[1024,256]{1,0:T(8,128)} %basis_ref.1), custom_call_target="tpu_custom_call" | custom-call | tf_op jit(solution)/shard_map/local_product/pallas_call | solution.py:71
  7.2 8.8 %collective-permute-start = (f32[8,32,8,256]{3,2,1,0:T(8,128)S(1)}, f32[8,32,8,256]{3,2,1,0:T(8,128)S(1)}, u32[]{:S(2)}, u32[]{:S(2)}) collective-permute-start(f32[8,32,8,256]{3,2,1,0:T(8,128)S(1)} %get-tuple-element.8), channel_id=1, source_target_pairs={{0,8},{1,9},{2,10},{3,11},{4,12},{5,13},{6,14},{7,15},{8,0},{9,1},... | collective-permute-start | bytes 6291464 | tf_op jit(solution)/shard_map/ppermute | solution.py:257
  16.0 3.8 %collective-permute-done = f32[8,32,8,256]{3,2,1,0:T(8,128)S(1)} collective-permute-done((f32[8,32,8,256]{3,2,1,0:T(8,128)S(1)}, f32[8,32,8,256]{3,2,1,0:T(8,128)S(1)}, u32[]{:S(2)}, u32[]{:S(2)}) %collective-permute-start) | collective-permute-done | bytes 2097184 | tf_op jit(solution)/shard_map/ppermute | solution.py:257
  19.7 0.3 add.3
  20.0 28.5 %all_to_all.25 = f32[8,32,8,256]{3,2,1,0:T(8,128)S(1)} all-to-all(f32[8,32,8,256]{3,2,1,0:T(8,128)S(1)} %add.3), channel_id=1, replica_groups=mesh['zh'=4,'zl'=2,'yh'=4,'core'=2,'yl'=2,'xh'=2,'xl'=2] {'zl','yl','xl'}, dimensions={0} | all-to-all | bytes 4194304 | tf_op jit(solution)/shard_map/all_to_all | solution.py:247
  48.5 0.1 reduce_sum.27
  48.6 28.0 %all_to_all.26 = f32[32,8,256]{2,1,0:T(8,128)S(1)} all-to-all(f32[32,8,256]{2,1,0:T(8,128)S(1)} %reduce_sum.27), channel_id=1, replica_groups=mesh['zh'=4,'zl'=2,'yh'=4,'core'=2,'yl'=2,'xh'=2,'xl'=2] {'zh','yh','xh'}, dimensions={0} | all-to-all | bytes 524288 | tf_op jit(solution)/shard_map/all_to_all | solution.py:247
  76.7 7.6 %all_to_all.27 = f32[8,8,256]{2,1,0:T(8,128)S(1)} all-to-all(f32[8,8,256]{2,1,0:T(8,128)S(1)} %broadcast_in_dim.6), channel_id=1, replica_groups=mesh['zh'=4,'zl'=2,'yh'=4,'core'=2,'yl'=2,'xh'=2,'xl'=2] {'yl','xh','xl'}, dimensions={0} | all-to-all | bytes 131072 | tf_op jit(solution)/shard_map/all_to_all | solution.py:247
  84.3 0.4 gram_terms.1
  84.7 23.2 %all_to_all.28 = f32[64,8,128]{2,1,0:T(8,128)S(1)} all-to-all(f32[64,8,128]{2,1,0:T(8,128)S(1)} %gram_terms.1), channel_id=1, replica_groups=mesh['zh'=4,'zl'=2,'yh'=4,'core'=2,'yl'=2,'xh'=2,'xl'=2] {'zh','zl','yh'..., dimensions={0} | all-to-all | bytes 524288 | tf_op jit(solution)/shard_map/all_to_all | solution.py:247
  107.9 0.1 reduce_sum.29
  108.0 19.7 %all_to_all.29.gram_ref = f32[64,8,128]{2,1,0:T(8,128)S(1)} all-to-all(f32[64,8,128]{2,1,0:T(8,128)S(1)} %broadcast_in_dim.7), channel_id=1, replica_groups=mesh['zh'=4,'zl'=2,'yh'=4,'core'=2,'yl'=2,'xh'=2,'xl'=2] {'zh','zl','yh'..., dimensions={0} | all-to-all | bytes 524288 | tf_op jit(solution)/shard_map/all_to_all | solution.py:247
  127.7 13.0 %finish.1 = f32[64,256]{1,0:T(8,128)} custom-call(f32[64,8,128]{2,1,0:T(8,128)S(1)} %all_to_all.29.gram_ref, f32[64,256]{1,0:T(8,128)S(1)} %bitcast.3), custom_call_target="tpu_custom_call" | custom-call | tf_op jit(solution)/shard_map/finish/pallas_call | solution.py:230
  (3 shorter events, 0.1 us)
Async XLA Ops:
  7.2 12.5 %collective-permute-start = (f32[8,32,8,256]{3,2,1,0:T(8,128)S(1)}, f32[8,32,8,256]{3,2,1,0:T(8,128)S(1)}, u32[]{:S(2)}, u32[]{:S(2)}) collective-permute-start(f32[8,32,8,256]{3,2,1,0:T(8,128)S(1)} %get-tuple-element.8), channel_id=1, source_target_pairs={{0,8},{1,9},{2,10},{3,11},{4,12},{5,13},{6,14},{7,15},{8,0},{9,1},... | collective-permute-start | bytes 6291464 | tf_op jit(solution)/shard_map/ppermute | solution.py:257

commit v3 on v2

--- a/solution.py
+++ b/solution.py
@@ -1,14 +1,17 @@
+import itertools
+import math
+
 import jax
 import jax.numpy as jnp
+import numpy as np
 from jax import lax
 from jax.experimental import pallas as pl
 from jax.experimental.pallas import tpu as pltpu
-from jax.sharding import Mesh
 from jax.sharding import PartitionSpec as P
 
 AXES = ("zh", "zl", "yh", "core", "yl", "xh", "xl")
 SIZES = (4, 2, 4, 2, 2, 2, 2)
-NEAR = ("zl", "yl", "xl")
+ALL = ("wide", "narrow")
 FAR = ("zh", "yh", "xh")
 WIDE = ("zh", "zl", "yh", "core")
 NARROW = ("yl", "xh", "xl")
@@ -243,8 +246,29 @@
     )(held(gram_tiles), held(rows))
 
 
-def exchange(x, axes):
-    return lax.all_to_all(x, axes, 0, 0, tiled=True)
+def members(axes):
+    index = np.arange(512).reshape(SIZES)
+    inner = [AXES.index(a) for a in axes]
+    outer = [i for i in range(len(AXES)) if i not in inner]
+    count = math.prod(SIZES[i] for i in inner)
+    return index.transpose(outer + inner).reshape(-1, count).tolist()
+
+
+def cubes():
+    groups = []
+    for core in range(2):
+        for z, y, x in itertools.product(range(0, 8, 2), range(0, 8, 2), range(0, 4, 2)):
+            group = [0] * 8
+            for dz, dy, dx in itertools.product(range(2), repeat=3):
+                at = ((z + core + dz) % 8, (y + core + dy) % 8, (x + core + dx) % 4)
+                place = (at[0] % 2) * 4 + (at[1] % 2) * 2 + at[2] % 2
+                group[place] = ((at[0] * 4 + at[1] // 2) * 2 + core) * 8 + (at[1] % 2) * 4 + at[2]
+            groups.append(group)
+    return groups
+
+
+def exchange(x, groups):
+    return lax.all_to_all(x, ALL, 0, 0, axis_index_groups=groups, tiled=True)
 
 
 def partner_pairs():
@@ -252,19 +276,18 @@
 
 
 def body(tile_values, tile_row, tile_col, basis):
-    core = lax.axis_index("core").astype(jnp.int32).reshape(1)
+    core = (lax.axis_index("wide").astype(jnp.int32) & 1).reshape(1)
+    wide, narrow = members(WIDE), members(NARROW)
     keep, send = local_product(tile_values, tile_row, tile_col, basis, core)
-    both = keep + lax.ppermute(send, AXES, partner_pairs())
-    over_near = jnp.sum(exchange(both, NEAR), axis=0)
-    rows = exchange(sum_and_spread(exchange(over_near, FAR), 8), NARROW).reshape(64, RANK)
-    terms = exchange(gram_terms(rows), WIDE)
-    gram_tiles = exchange(sum_and_spread(terms, 64), WIDE)
+    both = keep + lax.ppermute(send, ALL, partner_pairs())
+    over_near = jnp.sum(exchange(both, cubes()), axis=0)
+    rows = exchange(sum_and_spread(exchange(over_near, members(FAR)), 8), narrow).reshape(64, RANK)
+    terms = exchange(gram_terms(rows), wide)
+    gram_tiles = exchange(sum_and_spread(terms, 64), wide)
     return finish(gram_tiles, rows)
 
 
 def solution(mesh):
-    fine = Mesh(mesh.devices.reshape(SIZES), AXES)
-    in_specs = (P(AXES, None, None), P(AXES), P(AXES), P(AXES, None))
-    return jax.shard_map(
-        body, mesh=fine, in_specs=in_specs, out_specs=P(WIDE, None), check_vma=False
-    )
+    axes = mesh.axis_names
+    in_specs = (P(axes, None, None), P(axes), P(axes), P(axes, None))
+    return jax.shard_map(body, mesh=mesh, in_specs=in_specs, out_specs=P("wide", None), check_vma=False)

time: 141 us -> 133 us (0.943)
  blocking collectives: 107 us -> 99.2 us
    all_to_all x5, blocking collectives: 107 us -> 99.2 us  [exchange(): return lax.all_to_all(x, ALL, 0, 0, axis_index_groups=groups, tiled=True)]
where the time goes in v3:
time: 133 us
  blocking collectives  99.2 us (75%)
  Pallas kernels  20.6 us (15%)
  starting transfers between devices  8.75 us (7%)
  waiting for transfers between devices  3.76 us (3%)
    all_to_all x5, blocking collectives, exchange(): return lax.all_to_all(x, ALL, 0, 0, axis_index_groups=groups, tiled=True)  99.2 us
    pallas_call x1, Pallas kernels, finish(): pl.pallas_call(finish_kernel, in_specs=[IN_VMEM, IN_VMEM], out_shape=jax....  13 us
    ppermute x1, starting transfers between devices, body(): both = keep + lax.ppermute(send, ALL, partner_pairs())  8.75 us
    pallas_call x1, Pallas kernels, local_product(): pl.pallas_call(product_kernel, grid_spec=pltpu.PrefetchScalarGridSpec(num...  7.18 us
    ppermute x1, waiting for transfers between devices, body(): both = keep + lax.ppermute(send, ALL, partner_pairs())  3.76 us
  transfers between devices with their start and end apart: 1, of which 1 were waited for; matrix products, arithmetic and copies ran while one was open for 0% of the time, Pallas kernels for 0%

profile of v3, /device:TPU:1, one launch (start us, length us, event | category | flops | bytes accessed | tf_op | source)
XLA Modules:
  0.0 132.9 jit_solution(11409784681533277186)
XLA Ops:
  0.0 7.2 %local_product.1 = (f32[8,32,8,256]{3,2,1,0:T(8,128)S(1)}, f32[8,32,8,256]{3,2,1,0:T(8,128)S(1)}) custom-call(s32[7]{0:T(128)} %row_ref.1, s32[7]{0:T(128)} %col_ref.1, s32[1]{0:T(128)} %bitcast.core_ref, bf16[7,512,512]{2,1,0:T(8,128)(2,1)} %tile_ref.1, f32[1024,256]{1,0:T(8,128)} %basis_ref.1), custom_call_target="tpu_custom_call" | custom-call | tf_op jit(solution)/shard_map/local_product/pallas_call | solution.py:74
  7.2 8.8 %collective-permute-start = (f32[8,32,8,256]{3,2,1,0:T(8,128)S(1)}, f32[8,32,8,256]{3,2,1,0:T(8,128)S(1)}, u32[]{:S(2)}, u32[]{:S(2)}) collective-permute-start(f32[8,32,8,256]{3,2,1,0:T(8,128)S(1)} %get-tuple-element.8), channel_id=1, source_target_pairs={{0,8},{1,9},{2,10},{3,11},{4,12},{5,13},{6,14},{7,15},{8,0},{9,1},... | collective-permute-start | bytes 6291464 | tf_op jit(solution)/shard_map/ppermute | solution.py:282
  16.0 3.8 %collective-permute-done = f32[8,32,8,256]{3,2,1,0:T(8,128)S(1)} collective-permute-done((f32[8,32,8,256]{3,2,1,0:T(8,128)S(1)}, f32[8,32,8,256]{3,2,1,0:T(8,128)S(1)}, u32[]{:S(2)}, u32[]{:S(2)}) %collective-permute-start) | collective-permute-done | bytes 2097184 | tf_op jit(solution)/shard_map/ppermute | solution.py:282
  19.7 0.3 add.3
  20.0 28.9 %all_to_all.25 = f32[8,32,8,256]{3,2,1,0:T(8,128)S(1)} all-to-all(f32[8,32,8,256]{3,2,1,0:T(8,128)S(1)} %add.3), channel_id=1, replica_groups={{0,1,4,5,64,65,68,69},{2,3,6,7,66,67,70,71},{16,17,20,21,80,81,84,85},{..., dimensions={0} | all-to-all | bytes 4194304 | tf_op jit(solution)/shard_map/all_to_all | solution.py:271
  48.9 0.1 reduce_sum.27
  49.0 19.8 %all_to_all.26 = f32[32,8,256]{2,1,0:T(8,128)S(1)} all-to-all(f32[32,8,256]{2,1,0:T(8,128)S(1)} %reduce_sum.27), channel_id=1, replica_groups={{0,2,16,18,32,34,48,50,128,130,144,146,160,162,176,178,256,258,272,274,..., dimensions={0} | all-to-all | bytes 524288 | tf_op jit(solution)/shard_map/all_to_all | solution.py:271
  68.9 7.6 %all_to_all.27 = f32[8,8,256]{2,1,0:T(8,128)S(1)} all-to-all(f32[8,8,256]{2,1,0:T(8,128)S(1)} %broadcast_in_dim.6), channel_id=1, replica_groups={{0,1,2,3,4,5,6,7},{8,9,10,11,12,13,14,15},{16,17,18,19,20,21,22,23},{24..., dimensions={0} | all-to-all | bytes 131072 | tf_op jit(solution)/shard_map/all_to_all | solution.py:271
  76.5 0.4 gram_terms.1
  76.9 23.3 %all_to_all.28 = f32[64,8,128]{2,1,0:T(8,128)S(1)} all-to-all(f32[64,8,128]{2,1,0:T(8,128)S(1)} %gram_terms.1), channel_id=1, replica_groups={{0,8,16,24,32,40,48,56,64,72,80,88,96,104,112,120,128,136,144,152,160,1..., dimensions={0} | all-to-all | bytes 524288 | tf_op jit(solution)/shard_map/all_to_all | solution.py:271
  100.2 0.1 reduce_sum.29
  100.3 19.7 %all_to_all.29.gram_ref = f32[64,8,128]{2,1,0:T(8,128)S(1)} all-to-all(f32[64,8,128]{2,1,0:T(8,128)S(1)} %broadcast_in_dim.7), channel_id=1, replica_groups={{0,8,16,24,32,40,48,56,64,72,80,88,96,104,112,120,128,136,144,152,160,1..., dimensions={0} | all-to-all | bytes 524288 | tf_op jit(solution)/shard_map/all_to_all | solution.py:271
  119.9 13.0 %finish.1 = f32[64,256]{1,0:T(8,128)} custom-call(f32[64,8,128]{2,1,0:T(8,128)S(1)} %all_to_all.29.gram_ref, f32[64,256]{1,0:T(8,128)S(1)} %bitcast.3), custom_call_target="tpu_custom_call" | custom-call | tf_op jit(solution)/shard_map/finish/pallas_call | solution.py:233
  (3 shorter events, 0.1 us)
Async XLA Ops:
  7.2 12.5 %collective-permute-start = (f32[8,32,8,256]{3,2,1,0:T(8,128)S(1)}, f32[8,32,8,256]{3,2,1,0:T(8,128)S(1)}, u32[]{:S(2)}, u32[]{:S(2)}) collective-permute-start(f32[8,32,8,256]{3,2,1,0:T(8,128)S(1)} %get-tuple-element.8), channel_id=1, source_target_pairs={{0,8},{1,9},{2,10},{3,11},{4,12},{5,13},{6,14},{7,15},{8,0},{9,1},... | collective-permute-start | bytes 6291464 | tf_op jit(solution)/shard_map/ppermute | solution.py:282

commit v4 on v3

--- a/solution.py
+++ b/solution.py
@@ -13,8 +13,6 @@
 SIZES = (4, 2, 4, 2, 2, 2, 2)
 ALL = ("wide", "narrow")
 FAR = ("zh", "yh", "xh")
-WIDE = ("zh", "zl", "yh", "core")
-NARROW = ("yl", "xh", "xl")
 TILE = 512
 RANK = 256
 COLS = 4096
@@ -96,16 +94,13 @@
 
 def gram_kernel(rows_ref, out_ref):
     rows = rows_ref[...]
-    gram = lax.dot_general(
+    out_ref[...] = lax.dot_general(
         rows,
         rows,
         (((0,), (0,)), ((), ())),
         precision=HIGHEST,
         preferred_element_type=jnp.float32,
     )
-    for i in range(RANK // 8):
-        for h in range(2):
-            out_ref[2 * i + h] = gram[8 * i : 8 * i + 8, 128 * h : 128 * h + 128]
 
 
 def gram_terms(rows):
@@ -113,8 +108,8 @@
         gram_kernel,
         in_specs=[IN_VMEM],
         out_specs=IN_VMEM,
-        out_shape=pltpu.VMEM((64, 8, 128), jnp.float32),
-        compiler_params=pltpu.CompilerParams(vmem_limit_bytes=8 << 20),
+        out_shape=pltpu.VMEM((RANK, RANK), jnp.float32),
+        compiler_params=pltpu.CompilerParams(vmem_limit_bytes=24 << 20),
         name="gram_terms",
     )(held(rows))
 
@@ -175,11 +170,18 @@
     return out
 
 
-def finish_kernel(gram_ref, rows_ref, out_ref, s_ref, a_ref, u_ref, ua_ref, y_ref):
-    for i in range(RANK // 8):
-        for h in range(2):
-            s_ref[8 * i : 8 * i + 8, 128 * h : 128 * h + 128] = gram_ref[2 * i + h] * (1.0 / COLS)
-    rows = rows_ref[...]
+def finish_kernel(at_ref, gram_ref, other_ref, rows_ref, out_ref, s_ref, a_ref, u_ref, ua_ref, y_ref):
+    s_ref[...] = (gram_ref[...] + other_ref[...]) * (1.0 / COLS)
+    zl, far = at_ref[0], at_ref[1]
+    rows = jnp.concatenate(
+        [
+            rows_ref[zl * 4 + yl * 2 + xl, far + xh]
+            for yl in range(2)
+            for xh in range(2)
+            for xl in range(2)
+        ],
+        axis=0,
+    )
     a_ref[...] = jnp.concatenate([rows, jnp.zeros_like(rows)], axis=0).T
 
     def group(g, carry):
@@ -229,10 +231,10 @@
     out_ref[...] = y_ref[...].T[0:64, :]
 
 
-def finish(gram_tiles, rows):
+def finish(at, gram, other, rows):
     return pl.pallas_call(
         finish_kernel,
-        in_specs=[IN_VMEM, IN_VMEM],
+        in_specs=[pl.BlockSpec(memory_space=pltpu.SMEM), IN_VMEM, IN_VMEM, IN_VMEM],
         out_shape=jax.ShapeDtypeStruct((64, RANK), jnp.float32),
         scratch_shapes=[
             pltpu.VMEM((RANK, RANK), jnp.float32),
@@ -241,9 +243,9 @@
             pltpu.VMEM((SUPER, 128), jnp.float32),
             pltpu.VMEM((RANK, 128), jnp.float32),
         ],
-        compiler_params=pltpu.CompilerParams(vmem_limit_bytes=8 << 20),
+        compiler_params=pltpu.CompilerParams(vmem_limit_bytes=12 << 20),
         name="finish",
-    )(held(gram_tiles), held(rows))
+    )(at, held(gram), held(other), held(rows))
 
 
 def members(axes):
@@ -271,20 +273,22 @@
     return lax.all_to_all(x, ALL, 0, 0, axis_index_groups=groups, tiled=True)
 
 
-def partner_pairs():
-    return [(i, i ^ 8) for i in range(512)]
+PARTNERS = [(i, i ^ 8) for i in range(512)]
 
 
 def body(tile_values, tile_row, tile_col, basis):
-    core = (lax.axis_index("wide").astype(jnp.int32) & 1).reshape(1)
-    wide, narrow = members(WIDE), members(NARROW)
-    keep, send = local_product(tile_values, tile_row, tile_col, basis, core)
-    both = keep + lax.ppermute(send, ALL, partner_pairs())
-    over_near = jnp.sum(exchange(both, cubes()), axis=0)
-    rows = exchange(sum_and_spread(exchange(over_near, members(FAR)), 8), narrow).reshape(64, RANK)
-    terms = exchange(gram_terms(rows), wide)
-    gram_tiles = exchange(sum_and_spread(terms, 64), wide)
-    return finish(gram_tiles, rows)
+    wide = lax.axis_index("wide").astype(jnp.int32)
+    core, z, yh = wide & 1, wide >> 3, (wide >> 1) & 3
+    near, far = cubes(), members(FAR)
+    keep, send = local_product(tile_values, tile_row, tile_col, basis, core.reshape(1))
+    both = keep + lax.ppermute(send, ALL, PARTNERS)
+    over_near = jnp.sum(exchange(both, near), axis=0)
+    far_rows = exchange(sum_and_spread(exchange(over_near, far), 32), far)
+    rows = exchange(jnp.broadcast_to(far_rows, HALF), near)
+    gram = gram_terms(rows.reshape(COLS // 2, RANK))
+    other = lax.ppermute(gram, ALL, PARTNERS)
+    at = jnp.stack([z & 1, (z >> 1) * 8 + yh * 2])
+    return finish(at, gram, other, rows)
 
 
 def solution(mesh):

time: 133 us -> 131 us (0.985)
  blocking collectives: 99.2 us -> 91.3 us
  Pallas kernels: 20.6 us -> 22.8 us
  starting transfers between devices: 8.75 us -> 10.7 us
  waiting for transfers between devices: 3.76 us -> 5.18 us
    all_to_all x5 -> x4, blocking collectives: 99.2 us -> 91.3 us  [exchange(): return lax.all_to_all(x, ALL, 0, 0, axis_index_groups=groups, tiled=True)]
    ppermute x1 -> x2, starting transfers between devices: 8.75 us -> 10.7 us  [the longest x1 8.75 us: body(): both = keep + lax.ppermute(send, ALL, PARTNERS)]
    pallas_call x1, Pallas kernels: 0.41 us -> 2.1 us  [gram_terms(): pl.pallas_call(gram_kernel, in_specs=[IN_VMEM], out_specs=IN_VMEM, out_sh...]
    ppermute x1 -> x2, waiting for transfers between devices: 3.76 us -> 5.18 us  [the longest x1 3.76 us: body(): both = keep + lax.ppermute(send, ALL, PARTNERS)]
  transfers between devices with their start and end apart: 1 -> 2, of which waited for: 1 -> 2; matrix products, arithmetic and copies ran while one was open for 0% -> 0% of each run, Pallas kernels for 0% -> 0%
where the time goes in v4:
time: 131 us
  blocking collectives  91.3 us (70%)
  Pallas kernels  22.8 us (17%)
  starting transfers between devices  10.7 us (8%)
  waiting for transfers between devices  5.18 us (4%)
    all_to_all x4, blocking collectives, exchange(): return lax.all_to_all(x, ALL, 0, 0, axis_index_groups=groups, tiled=True)  91.3 us
    pallas_call x1, Pallas kernels, finish(): pl.pallas_call(finish_kernel, in_specs=[pl.BlockSpec(memory_space=pltpu.S...  13.6 us
    ppermute x1, starting transfers between devices, body(): both = keep + lax.ppermute(send, ALL, PARTNERS)  8.75 us
    pallas_call x1, Pallas kernels, local_product(): pl.pallas_call(product_kernel, grid_spec=pltpu.PrefetchScalarGridSpec(num...  7.18 us
    ppermute x1, waiting for transfers between devices, body(): both = keep + lax.ppermute(send, ALL, PARTNERS)  3.76 us
  transfers between devices with their start and end apart: 2, of which 2 were waited for; matrix products, arithmetic and copies ran while one was open for 0% of the time, Pallas kernels for 0%

profile of v4, /device:TPU:1, one launch (start us, length us, event | category | flops | bytes accessed | tf_op | source)
XLA Modules:
  0.0 130.8 jit_solution(11181833608304649656)
XLA Ops:
  0.0 7.2 %local_product.1 = (f32[8,32,8,256]{3,2,1,0:T(8,128)S(1)}, f32[8,32,8,256]{3,2,1,0:T(8,128)S(1)}) custom-call(s32[7]{0:T(128)} %row_ref.1, s32[7]{0:T(128)} %col_ref.1, s32[1]{0:T(128)} %bitcast.2.core_ref, bf16[7,512,512]{2,1,0:T(8,128)(2,1)} %tile_ref.1, f32[1024,256]{1,0:T(8,128)} %basis_ref.1), custom_call_target="tpu_custom_call" | custom-call | tf_op jit(solution)/shard_map/local_product/pallas_call | solution.py:72
  7.2 8.8 %collective-permute-start = (f32[8,32,8,256]{3,2,1,0:T(8,128)S(1)}, f32[8,32,8,256]{3,2,1,0:T(8,128)S(1)}, u32[]{:S(2)}, u32[]{:S(2)}) collective-permute-start(f32[8,32,8,256]{3,2,1,0:T(8,128)S(1)} %get-tuple-element.8), channel_id=1, source_target_pairs={{0,8},{1,9},{2,10},{3,11},{4,12},{5,13},{6,14},{7,15},{8,0},{9,1},... | collective-permute-start | bytes 6291464 | tf_op jit(solution)/shard_map/ppermute | solution.py:284
  16.0 3.8 %collective-permute-done = f32[8,32,8,256]{3,2,1,0:T(8,128)S(1)} collective-permute-done((f32[8,32,8,256]{3,2,1,0:T(8,128)S(1)}, f32[8,32,8,256]{3,2,1,0:T(8,128)S(1)}, u32[]{:S(2)}, u32[]{:S(2)}) %collective-permute-start) | collective-permute-done | bytes 2097184 | tf_op jit(solution)/shard_map/ppermute | solution.py:284
  19.7 0.3 add.7
  20.0 28.9 %all_to_all.20 = f32[8,32,8,256]{3,2,1,0:T(8,128)S(1)} all-to-all(f32[8,32,8,256]{3,2,1,0:T(8,128)S(1)} %add.7), channel_id=1, replica_groups={{0,1,4,5,64,65,68,69},{2,3,6,7,66,67,70,71},{16,17,20,21,80,81,84,85},{..., dimensions={0} | all-to-all | bytes 4194304 | tf_op jit(solution)/shard_map/all_to_all | solution.py:273
  48.9 0.1 reduce_sum.18
  49.0 19.8 %all_to_all.21 = f32[32,8,256]{2,1,0:T(8,128)S(1)} all-to-all(f32[32,8,256]{2,1,0:T(8,128)S(1)} %reduce_sum.18), channel_id=1, replica_groups={{0,2,16,18,32,34,48,50,128,130,144,146,160,162,176,178,256,258,272,274,..., dimensions={0} | all-to-all | bytes 524288 | tf_op jit(solution)/shard_map/all_to_all | solution.py:273
  68.9 20.9 %all_to_all.22 = f32[32,8,256]{2,1,0:T(8,128)S(1)} all-to-all(f32[32,8,256]{2,1,0:T(8,128)S(1)} %broadcast_in_dim.6), channel_id=1, replica_groups={{0,2,16,18,32,34,48,50,128,130,144,146,160,162,176,178,256,258,272,274,..., dimensions={0} | all-to-all | bytes 524288 | tf_op jit(solution)/shard_map/all_to_all | solution.py:273
  89.8 0.2 broadcast_in_dim.7
  90.0 21.8 %all_to_all.23.rows_ref = f32[8,32,8,256]{3,2,1,0:T(8,128)S(1)} all-to-all(f32[8,32,8,256]{3,2,1,0:T(8,128)S(1)} %broadcast_in_dim.7), channel_id=1, replica_groups={{0,1,4,5,64,65,68,69},{2,3,6,7,66,67,70,71},{16,17,20,21,80,81,84,85},{..., dimensions={0} | all-to-all | bytes 4194304 | tf_op jit(solution)/shard_map/all_to_all | solution.py:273
  111.7 2.1 %gram_terms.1.gram_ref = f32[256,256]{1,0:T(8,128)S(1)} custom-call(f32[2048,256]{1,0:T(8,128)S(1)} %bitcast.4), custom_call_target="tpu_custom_call" | custom-call | tf_op jit(solution)/shard_map/gram_terms/pallas_call | solution.py:107
  113.8 1.9 %collective-permute-start.1 = (f32[256,256]{1,0:T(8,128)S(1)}, f32[256,256]{1,0:T(8,128)S(1)}, u32[]{:S(2)}, u32[]{:S(2)}) collective-permute-start(f32[256,256]{1,0:T(8,128)S(1)} %gram_terms.1.gram_ref), channel_id=1, source_target_pairs={{0,8},{1,9},{2,10},{3,11},{4,12},{5,13},{6,14},{7,15},{8,0},{9,1},... | collective-permute-start | bytes 786440 | tf_op jit(solution)/shard_map/ppermute | solution.py:289
  115.8 0.1 pad_add_fusion.at_ref
  115.8 1.4 %collective-permute-done.1.other_ref = f32[256,256]{1,0:T(8,128)S(1)} collective-permute-done((f32[256,256]{1,0:T(8,128)S(1)}, f32[256,256]{1,0:T(8,128)S(1)}, u32[]{:S(2)}, u32[]{:S(2)}) %collective-permute-start.1) | collective-permute-done | bytes 262176 | tf_op jit(solution)/shard_map/ppermute | solution.py:289
  117.2 13.6 %finish.1 = f32[64,256]{1,0:T(8,128)} custom-call(s32[2]{0:T(128)S(1)} %pad_add_fusion.at_ref, f32[256,256]{1,0:T(8,128)S(1)} %gram_terms.1.gram_ref, f32[256,256]{1,0:T(8,128)S(1)} %collective-permute-done.1.other_ref, f32[8,32,8,256]{3,2,1,0:T(8,128)S(1)} %all_to_all.23.rows_ref), custom_call_target="tpu_custom_call" | custom-call | tf_op jit(solution)/shard_map/finish/pallas_call | solution.py:235
  (2 shorter events, 0.1 us)
Async XLA Ops:
  7.2 12.5 %collective-permute-start = (f32[8,32,8,256]{3,2,1,0:T(8,128)S(1)}, f32[8,32,8,256]{3,2,1,0:T(8,128)S(1)}, u32[]{:S(2)}, u32[]{:S(2)}) collective-permute-start(f32[8,32,8,256]{3,2,1,0:T(8,128)S(1)} %get-tuple-element.8), channel_id=1, source_target_pairs={{0,8},{1,9},{2,10},{3,11},{4,12},{5,13},{6,14},{7,15},{8,0},{9,1},... | collective-permute-start | bytes 6291464 | tf_op jit(solution)/shard_map/ppermute | solution.py:284
  113.8 3.4 %collective-permute-start.1 = (f32[256,256]{1,0:T(8,128)S(1)}, f32[256,256]{1,0:T(8,128)S(1)}, u32[]{:S(2)}, u32[]{:S(2)}) collective-permute-start(f32[256,256]{1,0:T(8,128)S(1)} %gram_terms.1.gram_ref), channel_id=1, source_target_pairs={{0,8},{1,9},{2,10},{3,11},{4,12},{5,13},{6,14},{7,15},{8,0},{9,1},... | collective-permute-start | bytes 786440 | tf_op jit(solution)/shard_map/ppermute | solution.py:289

commit v5 on v4

v5 whole, which is shorter than its diff:
```python
import itertools
import math

import jax
import jax.numpy as jnp
import numpy as np
from jax import lax
from jax.experimental import pallas as pl
from jax.experimental.pallas import tpu as pltpu
from jax.sharding import PartitionSpec as P

AXES = ("zh", "zl", "yh", "core", "yl", "xh", "xl")
SIZES = (4, 2, 4, 2, 2, 2, 2)
ALL = ("wide", "narrow")
FAR = ("zh", "yh", "xh")
TILE = 512
RANK = 256
COLS = 4096
HIGHEST = lax.Precision.HIGHEST
HALF = (8, 32, 8, RANK)
IN_VMEM = pl.BlockSpec(memory_space=pltpu.VMEM)


def held(x):
    return pltpu.with_memory_space_constraint(x, pltpu.VMEM)


def left_out(x):
    return pltpu.with_memory_space_constraint(x, pltpu.HBM)


def product_kernel(row_ref, col_ref, core_ref, tile_ref, basis_ref, keep_ref, send_ref, tiles, rows, rounded, tile_sem, row_sem):
    count = tiles.shape[0]
    rows_in = pltpu.make_async_copy(basis_ref, rows, row_sem)
    rows_in.start()
    for t in range(count):
        pltpu.make_async_copy(tile_ref.at[t], tiles.at[t], tile_sem.at[t]).start()
    keep_ref[...] = jnp.zeros_like(keep_ref)
    send_ref[...] = jnp.zeros_like(send_ref)
    rows_in.wait()
    rounded[...] = rows[...].astype(jnp.bfloat16).reshape(rounded.shape)

    def step(t, carry):
        pltpu.make_async_copy(tile_ref.at[t], tiles.at[t], tile_sem.at[t]).wait()
        c = col_ref[t]
        near, far = (c & 1) * 4, (c >> 1) * 8
        res = lax.dot_general(
            tiles[t],
            rounded[row_ref[t]],
            (((0,), (0,)), ((), ())),
            preferred_element_type=jnp.float32,
        )

        def add(halves):
            for yh in range(4):
                for core in range(2):
                    for yl in range(2):
                        for xh in range(2):
                            for xl in range(2):
                                i = (((yh * 2 + core) * 2 + yl) * 2 + xh) * 2 + xl
                                halves[core][near + yl * 2 + xl, far + yh * 2 + xh] += res[8 * i : 8 * i + 8, :]

        @pl.when(core_ref[0] == 0)
        def _():
            add((keep_ref, send_ref))

        @pl.when(core_ref[0] == 1)
        def _():
            add((send_ref, keep_ref))

        return carry

    lax.fori_loop(0, count, step, 0)


def local_product(tile_values, tile_row, tile_col, basis, core):
    tiles = tile_values.shape[0]
    blocks = basis.shape[0] // TILE
    outside = pl.BlockSpec(memory_space=pltpu.HBM)
    return pl.pallas_call(
        product_kernel,
        grid_spec=pltpu.PrefetchScalarGridSpec(
            num_scalar_prefetch=3,
            grid=(),
            in_specs=[outside, outside],
            out_specs=[IN_VMEM, IN_VMEM],
            scratch_shapes=[
                pltpu.VMEM(tile_values.shape, tile_values.dtype),
                pltpu.VMEM(basis.shape, basis.dtype),
                pltpu.VMEM((blocks, TILE, RANK), jnp.bfloat16),
                pltpu.SemaphoreType.DMA((tiles,)),
                pltpu.SemaphoreType.DMA,
            ],
        ),
        out_shape=[pltpu.VMEM(HALF, jnp.float32)] * 2,
        compiler_params=pltpu.CompilerParams(vmem_limit_bytes=16 << 20),
        name="local_product",
    )(left_out(tile_row), left_out(tile_col), core, left_out(tile_values), left_out(basis))


def sum_and_spread(parts, copies):
    total = jnp.sum(parts, axis=0)
    return jnp.broadcast_to(total, (copies,) + total.shape)


def gram_kernel(rows_ref, out_ref):
    rows = rows_ref[...]
    out_ref[...] = lax.dot_general(
        rows,
        rows,
        (((0,), (0,)), ((), ())),
        precision=HIGHEST,
        preferred_element_type=jnp.float32,
    )


def gram_terms(rows):
    return pl.pallas_call(
        gram_kernel,
        in_specs=[IN_VMEM],
        out_specs=IN_VMEM,
        out_shape=pltpu.VMEM((RANK, RANK), jnp.float32),
        compiler_params=pltpu.CompilerParams(vmem_limit_bytes=24 << 20),
        name="gram_terms",
    )(held(rows))


def lane(v, j):
    return jnp.broadcast_to(v[:, j : j + 1], (8, 128))


def sub(v, i):
    return jnp.broadcast_to(v[i : i + 1, :], v.shape)


def total(terms):
    while len(terms) > 1:
        terms = [x + y for x, y in zip(terms[::2], terms[1::2])] + terms[len(terms) & ~1 :]
    return terms[0]


def invert_factor(block, at):
    e = {}
    for j in range(8):
        column = lane(block, at + j)
        for i in range(j, 8):
            e[i, j] = sub(column, i)
    inv = {}
    for j in range(8):
        r = lax.rsqrt(e[j, j])
        inv[j, j] = r
        for i in range(j + 1, 8):
            e[i, j] = e[i, j] * r
        for k in range(j + 1, 8):
            for i in range(k, 8):
                e[i, k] = e[i, k] - e[i, j] * e[k, j]
        for k in range(j):
            inv[j, k] = -r * total([e[j, i] * inv[i, k] for i in range(k, j)])
    place = lax.broadcasted_iota(jnp.int32, (8, 128), 0)
    zero = jnp.zeros((8, 128), jnp.float32)
    lower, upper = [], []
    for j in range(8):
        down = across = zero
        for i in range(j, 8):
            down = jnp.where(place == i, inv[i, j], down)
        for i in range(j + 1):
            across = jnp.where(place == i, inv[j, i], across)
        lower.append(down)
        upper.append(across)
    return lower, upper


def combine(columns, rows):
    return [total([columns[j] * sub(piece, j) for j in range(8)]) for piece in rows]


def eliminate(refs, first):
    for k in range(16):
        here = slice(first + 8 * k, first + 8 * k + 8)
        pieces = [ref[here, :] for ref in refs]
        lower, upper = invert_factor(pieces[0], 8 * k)
        scaled = combine(lower, pieces)
        for ref, piece in zip(refs[1:], scaled[1:]):
            ref[here, :] = piece
        if k == 15:
            break
        solved = combine(upper, scaled)
        solved = [[sub(piece, j) for j in range(8)] for piece in solved]
        for q in range(k + 1, 16):
            there = slice(first + 8 * q, first + 8 * q + 8)
            old = [ref[there, :] for ref in refs]
            ms = [lane(old[0], 8 * k + j) for j in range(8)]
            for ref, piece, by in zip(refs, old, solved):
                ref[there, :] = piece - total([ms[j] * by[j] for j in range(8)])


def finish_kernel(at_ref, gram_ref, other_ref, rows_ref, out_ref, left_ref, right_ref, y_ref):
    s = (gram_ref[...] + other_ref[...]) * (1.0 / COLS)
    left_ref[...] = s[:, 0:128]
    right_ref[...] = s[:, 128:256]
    zl, far = at_ref[0], at_ref[1]
    rows = jnp.concatenate(
        [
            rows_ref[zl * 4 + yl * 2 + xl, far + xh]
            for yl in range(2)
            for xh in range(2)
            for xl in range(2)
        ],
        axis=0,
    )
    y_ref[...] = jnp.concatenate([rows, jnp.zeros_like(rows)], axis=0).T
    eliminate((left_ref, right_ref, y_ref), 0)
    u, ua = right_ref[0:128, :], y_ref[0:128, :]
    for ref, by in ((right_ref, u), (y_ref, ua)):
        ref[128:256, :] -= lax.dot_general(
            u, by, (((0,), (0,)), ((), ())), precision=HIGHEST, preferred_element_type=jnp.float32
        )
    eliminate((right_ref, y_ref), 128)
    out_ref[...] = y_ref[...].T[0:64, :]


def finish(at, gram, other, rows):
    return pl.pallas_call(
        finish_kernel,
        in_specs=[pl.BlockSpec(memory_space=pltpu.SMEM), IN_VMEM, IN_VMEM, IN_VMEM],
        out_shape=jax.ShapeDtypeStruct((64, RANK), jnp.float32),
        scratch_shapes=[pltpu.VMEM((RANK, 128), jnp.float32)] * 3,
        compiler_params=pltpu.CompilerParams(vmem_limit_bytes=12 << 20),
        name="finish",
    )(at, held(gram), held(other), held(rows))


def members(axes):
    index = np.arange(512).reshape(SIZES)
    inner = [AXES.index(a) for a in axes]
    outer = [i for i in range(len(AXES)) if i not in inner]
    count = math.prod(SIZES[i] for i in inner)
    return index.transpose(outer + inner).reshape(-1, count).tolist()


def cubes():
    groups = []
    for core in range(2):
        for z, y, x in itertools.product(range(0, 8, 2), range(0, 8, 2), range(0, 4, 2)):
            group = [0] * 8
            for dz, dy, dx in itertools.product(range(2), repeat=3):
                at = ((z + core + dz) % 8, (y + core + dy) % 8, (x + core + dx) % 4)
                place = (at[0] % 2) * 4 + (at[1] % 2) * 2 + at[2] % 2
                group[place] = ((at[0] * 4 + at[1] // 2) * 2 + core) * 8 + (at[1] % 2) * 4 + at[2]
            groups.append(group)
    return groups


def exchange(x, groups):
    return lax.all_to_all(x, ALL, 0, 0, axis_index_groups=groups, tiled=True)


PARTNERS = [(i, i ^ 8) for i in range(512)]


def body(tile_values, tile_row, tile_col, basis):
    wide = lax.axis_index("wide").astype(jnp.int32)
    core, z, yh = wide & 1, wide >> 3, (wide >> 1) & 3
    near, far = cubes(), members(FAR)
    keep, send = local_product(tile_values, tile_row, tile_col, basis, core.reshape(1))
    both = keep + lax.ppermute(send, ALL, PARTNERS)
    over_near = jnp.sum(exchange(both, near), axis=0)
    far_rows = exchange(sum_and_spread(exchange(over_near, far), 32), far)
    rows = exchange(jnp.broadcast_to(far_rows, HALF), near)
    gram = gram_terms(rows.reshape(COLS // 2, RANK))
    other = lax.ppermute(gram, ALL, PARTNERS)
    at = jnp.stack([z & 1, (z >> 1) * 8 + yh * 2])
    return finish(at, gram, other, rows)


def solution(mesh):
    axes = mesh.axis_names
    in_specs = (P(axes, None, None), P(axes), P(axes), P(axes, None))
    return jax.shard_map(body, mesh=mesh, in_specs=in_specs, out_specs=P("wide", None), check_vma=False)
```

time: 131 us -> 127 us (0.969)
  Pallas kernels: 22.8 us -> 19 us
    pallas_call x1, Pallas kernels: 13.6 us -> 11.1 us  [finish(): pl.pallas_call(finish_kernel, in_specs=[pl.BlockSpec(memory_space=pltpu.S...]
    pallas_call x1, Pallas kernels: 7.18 us -> 5.8 us  [local_product(): pl.pallas_call(product_kernel, grid_spec=pltpu.PrefetchScalarGridSpec(num...]
where the time goes in v5:
time: 127 us
  blocking collectives  91.3 us (72%)
  Pallas kernels  19 us (15%)
  starting transfers between devices  10.8 us (9%)
  waiting for transfers between devices  5 us (4%)
    all_to_all x4, blocking collectives, exchange(): return lax.all_to_all(x, ALL, 0, 0, axis_index_groups=groups, tiled=True)  91.3 us
    pallas_call x1, Pallas kernels, finish(): pl.pallas_call(finish_kernel, in_specs=[pl.BlockSpec(memory_space=pltpu.S...  11.1 us
    ppermute x1, starting transfers between devices, body(): both = keep + lax.ppermute(send, ALL, PARTNERS)  8.75 us
    pallas_call x1, Pallas kernels, local_product(): pl.pallas_call(product_kernel, grid_spec=pltpu.PrefetchScalarGridSpec(num...  5.8 us
    ppermute x1, waiting for transfers between devices, body(): both = keep + lax.ppermute(send, ALL, PARTNERS)  3.76 us
  transfers between devices with their start and end apart: 2, of which 2 were waited for; matrix products, arithmetic and copies ran while one was open for 0% of the time, Pallas kernels for 0%

profile of v5, /device:TPU:1, one launch (start us, length us, event | category | flops | bytes accessed | tf_op | source)
XLA Modules:
  0.0 126.9 jit_solution(4968131088336557858)
XLA Ops:
  0.0 5.8 %local_product.1 = (f32[8,32,8,256]{3,2,1,0:T(8,128)S(1)}, f32[8,32,8,256]{3,2,1,0:T(8,128)S(1)}) custom-call(s32[7]{0:T(128)} %row_ref.1, s32[7]{0:T(128)} %col_ref.1, s32[1]{0:T(128)} %bitcast.2.core_ref, bf16[7,512,512]{2,1,0:T(8,128)(2,1)} %tile_ref.1, f32[1024,256]{1,0:T(8,128)} %basis_ref.1), custom_call_target="tpu_custom_call" | custom-call | tf_op jit(solution)/shard_map/local_product/pallas_call | solution.py:80
  5.8 8.7 %collective-permute-start = (f32[8,32,8,256]{3,2,1,0:T(8,128)S(1)}, f32[8,32,8,256]{3,2,1,0:T(8,128)S(1)}, u32[]{:S(2)}, u32[]{:S(2)}) collective-permute-start(f32[8,32,8,256]{3,2,1,0:T(8,128)S(1)} %get-tuple-element.8), channel_id=1, source_target_pairs={{0,8},{1,9},{2,10},{3,11},{4,12},{5,13},{6,14},{7,15},{8,0},{9,1},... | collective-permute-start | bytes 6291464 | tf_op jit(solution)/shard_map/ppermute | solution.py:266
  14.6 3.8 %collective-permute-done = f32[8,32,8,256]{3,2,1,0:T(8,128)S(1)} collective-permute-done((f32[8,32,8,256]{3,2,1,0:T(8,128)S(1)}, f32[8,32,8,256]{3,2,1,0:T(8,128)S(1)}, u32[]{:S(2)}, u32[]{:S(2)}) %collective-permute-start) | collective-permute-done | bytes 2097184 | tf_op jit(solution)/shard_map/ppermute | solution.py:266
  18.3 0.3 add.7
  18.6 28.9 %all_to_all.20 = f32[8,32,8,256]{3,2,1,0:T(8,128)S(1)} all-to-all(f32[8,32,8,256]{3,2,1,0:T(8,128)S(1)} %add.7), channel_id=1, replica_groups={{0,1,4,5,64,65,68,69},{2,3,6,7,66,67,70,71},{16,17,20,21,80,81,84,85},{..., dimensions={0} | all-to-all | bytes 4194304 | tf_op jit(solution)/shard_map/all_to_all | solution.py:255
  47.5 0.1 reduce_sum.18
  47.6 19.8 %all_to_all.21 = f32[32,8,256]{2,1,0:T(8,128)S(1)} all-to-all(f32[32,8,256]{2,1,0:T(8,128)S(1)} %reduce_sum.18), channel_id=1, replica_groups={{0,2,16,18,32,34,48,50,128,130,144,146,160,162,176,178,256,258,272,274,..., dimensions={0} | all-to-all | bytes 524288 | tf_op jit(solution)/shard_map/all_to_all | solution.py:255
  67.5 20.9 %all_to_all.22 = f32[32,8,256]{2,1,0:T(8,128)S(1)} all-to-all(f32[32,8,256]{2,1,0:T(8,128)S(1)} %broadcast_in_dim.6), channel_id=1, replica_groups={{0,2,16,18,32,34,48,50,128,130,144,146,160,162,176,178,256,258,272,274,..., dimensions={0} | all-to-all | bytes 524288 | tf_op jit(solution)/shard_map/all_to_all | solution.py:255
  88.4 0.2 broadcast_in_dim.7
  88.6 21.8 %all_to_all.23.rows_ref = f32[8,32,8,256]{3,2,1,0:T(8,128)S(1)} all-to-all(f32[8,32,8,256]{3,2,1,0:T(8,128)S(1)} %broadcast_in_dim.7), channel_id=1, replica_groups={{0,1,4,5,64,65,68,69},{2,3,6,7,66,67,70,71},{16,17,20,21,80,81,84,85},{..., dimensions={0} | all-to-all | bytes 4194304 | tf_op jit(solution)/shard_map/all_to_all | solution.py:255
  110.3 2.1 %gram_terms.1.gram_ref = f32[256,256]{1,0:T(8,128)S(1)} custom-call(f32[2048,256]{1,0:T(8,128)S(1)} %bitcast.4), custom_call_target="tpu_custom_call" | custom-call | tf_op jit(solution)/shard_map/gram_terms/pallas_call | solution.py:118
  112.4 2.1 %collective-permute-start.1 = (f32[256,256]{1,0:T(8,128)S(1)}, f32[256,256]{1,0:T(8,128)S(1)}, u32[]{:S(2)}, u32[]{:S(2)}) collective-permute-start(f32[256,256]{1,0:T(8,128)S(1)} %gram_terms.1.gram_ref), channel_id=1, source_target_pairs={{0,8},{1,9},{2,10},{3,11},{4,12},{5,13},{6,14},{7,15},{8,0},{9,1},... | collective-permute-start | bytes 786440 | tf_op jit(solution)/shard_map/ppermute | solution.py:271
  114.5 0.1 pad_add_fusion.at_ref
  114.6 1.2 collective-permute-done.1.other_ref
  115.9 11.1 %finish.1 = f32[64,256]{1,0:T(8,128)} custom-call(s32[2]{0:T(128)S(1)} %pad_add_fusion.at_ref, f32[256,256]{1,0:T(8,128)S(1)} %gram_terms.1.gram_ref, f32[256,256]{1,0:T(8,128)S(1)} %collective-permute-done.1.other_ref, f32[8,32,8,256]{3,2,1,0:T(8,128)S(1)} %all_to_all.23.rows_ref), custom_call_target="tpu_custom_call" | custom-call | tf_op jit(solution)/shard_map/finish/pallas_call | solution.py:223
  (2 shorter events, 0.1 us)
Async XLA Ops:
  5.8 12.5 %collective-permute-start = (f32[8,32,8,256]{3,2,1,0:T(8,128)S(1)}, f32[8,32,8,256]{3,2,1,0:T(8,128)S(1)}, u32[]{:S(2)}, u32[]{:S(2)}) collective-permute-start(f32[8,32,8,256]{3,2,1,0:T(8,128)S(1)} %get-tuple-element.8), channel_id=1, source_target_pairs={{0,8},{1,9},{2,10},{3,11},{4,12},{5,13},{6,14},{7,15},{8,0},{9,1},... | collective-permute-start | bytes 6291464 | tf_op jit(solution)/shard_map/ppermute | solution.py:266
  112.4 3.4 %collective-permute-start.1 = (f32[256,256]{1,0:T(8,128)S(1)}, f32[256,256]{1,0:T(8,128)S(1)}, u32[]{:S(2)}, u32[]{:S(2)}) collective-permute-start(f32[256,256]{1,0:T(8,128)S(1)} %gram_terms.1.gram_ref), channel_id=1, source_target_pairs={{0,8},{1,9},{2,10},{3,11},{4,12},{5,13},{6,14},{7,15},{8,0},{9,1},... | collective-permute-start | bytes 786440 | tf_op jit(solution)/shard_map/ppermute | solution.py:271

commit v6 on v5

--- a/solution.py
+++ b/solution.py
@@ -141,10 +141,10 @@
 
 def invert_factor(block, at):
     e = {}
-    for j in range(8):
-        column = lane(block, at + j)
-        for i in range(j, 8):
-            e[i, j] = sub(column, i)
+    for i in range(8):
+        row = sub(block, i)
+        for j in range(i + 1):
+            e[i, j] = lane(row, at + j)
     inv = {}
     for j in range(8):
         r = lax.rsqrt(e[j, j])
@@ -167,7 +167,7 @@
             across = jnp.where(place == i, inv[j, i], across)
         lower.append(down)
         upper.append(across)
-    return lower, upper
+    return lower, upper, inv
 
 
 def combine(columns, rows):
@@ -178,20 +178,24 @@
     for k in range(16):
         here = slice(first + 8 * k, first + 8 * k + 8)
         pieces = [ref[here, :] for ref in refs]
-        lower, upper = invert_factor(pieces[0], 8 * k)
+        lower, upper, inverse = invert_factor(pieces[0], 8 * k)
         scaled = combine(lower, pieces)
         for ref, piece in zip(refs[1:], scaled[1:]):
             ref[here, :] = piece
         if k == 15:
             break
-        solved = combine(upper, scaled)
-        solved = [[sub(piece, j) for j in range(8)] for piece in solved]
-        for q in range(k + 1, 16):
-            there = slice(first + 8 * q, first + 8 * q + 8)
-            old = [ref[there, :] for ref in refs]
-            ms = [lane(old[0], 8 * k + j) for j in range(8)]
-            for ref, piece, by in zip(refs, old, solved):
-                ref[there, :] = piece - total([ms[j] * by[j] for j in range(8)])
+        there = slice(first + 8 * (k + 1), first + 8 * (k + 2))
+        old = [ref[there, :] for ref in refs]
+        ms = [lane(old[0], 8 * k + j) for j in range(8)]
+        factor = [total([ms[i] * inverse[j, i] for i in range(j + 1)]) for j in range(8)]
+        for ref, piece, by in zip(refs, old, scaled):
+            ref[there, :] = piece - total([factor[j] * sub(by, j) for j in range(8)])
+        if k + 2 < 16:
+            solved = combine(upper, scaled)
+            there = slice(first + 8 * (k + 2), first + 128)
+            left = refs[0][there, 8 * k : 8 * k + 8]
+            for ref, piece in zip(refs, solved):
+                ref[there, :] -= jnp.dot(left, piece, precision=HIGHEST, preferred_element_type=jnp.float32)
 
 
 def finish_kernel(at_ref, gram_ref, other_ref, rows_ref, out_ref, left_ref, right_ref, y_ref):

time: 127 us -> 126 us (level)
  no operation moved by 1% of the time
where the time goes in v6:
time: 126 us
  blocking collectives  91.3 us (72%)
  Pallas kernels  18 us (14%)
  starting transfers between devices  10.8 us (9%)
  waiting for transfers between devices  5 us (4%)
    all_to_all x4, blocking collectives, exchange(): return lax.all_to_all(x, ALL, 0, 0, axis_index_groups=groups, tiled=True)  91.3 us
    pallas_call x1, Pallas kernels, finish(): pl.pallas_call(finish_kernel, in_specs=[pl.BlockSpec(memory_space=pltpu.S...  10.1 us
    ppermute x1, starting transfers between devices, body(): both = keep + lax.ppermute(send, ALL, PARTNERS)  8.75 us
    pallas_call x1, Pallas kernels, local_product(): pl.pallas_call(product_kernel, grid_spec=pltpu.PrefetchScalarGridSpec(num...  5.8 us
    ppermute x1, waiting for transfers between devices, body(): both = keep + lax.ppermute(send, ALL, PARTNERS)  3.76 us
  transfers between devices with their start and end apart: 2, of which 2 were waited for; matrix products, arithmetic and copies ran while one was open for 0% of the time, Pallas kernels for 0%

profile of v6, /device:TPU:1, one launch (start us, length us, event | category | flops | bytes accessed | tf_op | source)
XLA Modules:
  0.0 126.0 jit_solution(9179063102591910847)
XLA Ops:
  0.0 5.8 %local_product.1 = (f32[8,32,8,256]{3,2,1,0:T(8,128)S(1)}, f32[8,32,8,256]{3,2,1,0:T(8,128)S(1)}) custom-call(s32[7]{0:T(128)} %row_ref.1, s32[7]{0:T(128)} %col_ref.1, s32[1]{0:T(128)} %bitcast.2.core_ref, bf16[7,512,512]{2,1,0:T(8,128)(2,1)} %tile_ref.1, f32[1024,256]{1,0:T(8,128)} %basis_ref.1), custom_call_target="tpu_custom_call" | custom-call | tf_op jit(solution)/shard_map/local_product/pallas_call | solution.py:80
  5.8 8.7 %collective-permute-start = (f32[8,32,8,256]{3,2,1,0:T(8,128)S(1)}, f32[8,32,8,256]{3,2,1,0:T(8,128)S(1)}, u32[]{:S(2)}, u32[]{:S(2)}) collective-permute-start(f32[8,32,8,256]{3,2,1,0:T(8,128)S(1)} %get-tuple-element.8), channel_id=1, source_target_pairs={{0,8},{1,9},{2,10},{3,11},{4,12},{5,13},{6,14},{7,15},{8,0},{9,1},... | collective-permute-start | bytes 6291464 | tf_op jit(solution)/shard_map/ppermute | solution.py:270
  14.6 3.8 %collective-permute-done = f32[8,32,8,256]{3,2,1,0:T(8,128)S(1)} collective-permute-done((f32[8,32,8,256]{3,2,1,0:T(8,128)S(1)}, f32[8,32,8,256]{3,2,1,0:T(8,128)S(1)}, u32[]{:S(2)}, u32[]{:S(2)}) %collective-permute-start) | collective-permute-done | bytes 2097184 | tf_op jit(solution)/shard_map/ppermute | solution.py:270
  18.3 0.3 add.7
  18.6 28.9 %all_to_all.20 = f32[8,32,8,256]{3,2,1,0:T(8,128)S(1)} all-to-all(f32[8,32,8,256]{3,2,1,0:T(8,128)S(1)} %add.7), channel_id=1, replica_groups={{0,1,4,5,64,65,68,69},{2,3,6,7,66,67,70,71},{16,17,20,21,80,81,84,85},{..., dimensions={0} | all-to-all | bytes 4194304 | tf_op jit(solution)/shard_map/all_to_all | solution.py:259
  47.5 0.1 reduce_sum.18
  47.6 19.8 %all_to_all.21 = f32[32,8,256]{2,1,0:T(8,128)S(1)} all-to-all(f32[32,8,256]{2,1,0:T(8,128)S(1)} %reduce_sum.18), channel_id=1, replica_groups={{0,2,16,18,32,34,48,50,128,130,144,146,160,162,176,178,256,258,272,274,..., dimensions={0} | all-to-all | bytes 524288 | tf_op jit(solution)/shard_map/all_to_all | solution.py:259
  67.5 20.9 %all_to_all.22 = f32[32,8,256]{2,1,0:T(8,128)S(1)} all-to-all(f32[32,8,256]{2,1,0:T(8,128)S(1)} %broadcast_in_dim.6), channel_id=1, replica_groups={{0,2,16,18,32,34,48,50,128,130,144,146,160,162,176,178,256,258,272,274,..., dimensions={0} | all-to-all | bytes 524288 | tf_op jit(solution)/shard_map/all_to_all | solution.py:259
  88.4 0.2 broadcast_in_dim.7
  88.6 21.8 %all_to_all.23.rows_ref = f32[8,32,8,256]{3,2,1,0:T(8,128)S(1)} all-to-all(f32[8,32,8,256]{3,2,1,0:T(8,128)S(1)} %broadcast_in_dim.7), channel_id=1, replica_groups={{0,1,4,5,64,65,68,69},{2,3,6,7,66,67,70,71},{16,17,20,21,80,81,84,85},{..., dimensions={0} | all-to-all | bytes 4194304 | tf_op jit(solution)/shard_map/all_to_all | solution.py:259
  110.3 2.1 %gram_terms.1.gram_ref = f32[256,256]{1,0:T(8,128)S(1)} custom-call(f32[2048,256]{1,0:T(8,128)S(1)} %bitcast.4), custom_call_target="tpu_custom_call" | custom-call | tf_op jit(solution)/shard_map/gram_terms/pallas_call | solution.py:118
  112.4 2.1 %collective-permute-start.1 = (f32[256,256]{1,0:T(8,128)S(1)}, f32[256,256]{1,0:T(8,128)S(1)}, u32[]{:S(2)}, u32[]{:S(2)}) collective-permute-start(f32[256,256]{1,0:T(8,128)S(1)} %gram_terms.1.gram_ref), channel_id=1, source_target_pairs={{0,8},{1,9},{2,10},{3,11},{4,12},{5,13},{6,14},{7,15},{8,0},{9,1},... | collective-permute-start | bytes 786440 | tf_op jit(solution)/shard_map/ppermute | solution.py:275
  114.5 0.1 pad_add_fusion.at_ref
  114.6 1.2 collective-permute-done.1.other_ref
  115.9 10.1 %finish.1 = f32[64,256]{1,0:T(8,128)} custom-call(s32[2]{0:T(128)S(1)} %pad_add_fusion.at_ref, f32[256,256]{1,0:T(8,128)S(1)} %gram_terms.1.gram_ref, f32[256,256]{1,0:T(8,128)S(1)} %collective-permute-done.1.other_ref, f32[8,32,8,256]{3,2,1,0:T(8,128)S(1)} %all_to_all.23.rows_ref), custom_call_target="tpu_custom_call" | custom-call | tf_op jit(solution)/shard_map/finish/pallas_call | solution.py:227
  (2 shorter events, 0.1 us)
Async XLA Ops:
  5.8 12.5 %collective-permute-start = (f32[8,32,8,256]{3,2,1,0:T(8,128)S(1)}, f32[8,32,8,256]{3,2,1,0:T(8,128)S(1)}, u32[]{:S(2)}, u32[]{:S(2)}) collective-permute-start(f32[8,32,8,256]{3,2,1,0:T(8,128)S(1)} %get-tuple-element.8), channel_id=1, source_target_pairs={{0,8},{1,9},{2,10},{3,11},{4,12},{5,13},{6,14},{7,15},{8,0},{9,1},... | collective-permute-start | bytes 6291464 | tf_op jit(solution)/shard_map/ppermute | solution.py:270
  112.4 3.4 %collective-permute-start.1 = (f32[256,256]{1,0:T(8,128)S(1)}, f32[256,256]{1,0:T(8,128)S(1)}, u32[]{:S(2)}, u32[]{:S(2)}) collective-permute-start(f32[256,256]{1,0:T(8,128)S(1)} %gram_terms.1.gram_ref), channel_id=1, source_target_pairs={{0,8},{1,9},{2,10},{3,11},{4,12},{5,13},{6,14},{7,15},{8,0},{9,1},... | collective-permute-start | bytes 786440 | tf_op jit(solution)/shard_map/ppermute | solution.py:275

commit v7 on v6

--- a/solution.py
+++ b/solution.py
@@ -104,14 +104,15 @@
 
 
 def gram_kernel(rows_ref, out_ref):
-    rows = rows_ref[...]
-    out_ref[...] = lax.dot_general(
-        rows,
-        rows,
-        (((0,), (0,)), ((), ())),
-        precision=HIGHEST,
-        preferred_element_type=jnp.float32,
-    )
+    def inner(a, b):
+        return lax.dot_general(
+            a, b, (((0,), (0,)), ((), ())), precision=HIGHEST, preferred_element_type=jnp.float32
+        )
+
+    left, right = rows_ref[:, 0:128], rows_ref[:, 128:256]
+    out_ref[0:128, :] = inner(left, rows_ref[...])
+    out_ref[128:256, 0:128] = out_ref[0:128, 128:256].T
+    out_ref[128:256, 128:256] = inner(right, right)
 
 
 def gram_terms(rows):

time: 126 us -> 126 us (level)
  no operation moved by 1% of the time
where the time goes in v7:
time: 126 us
  blocking collectives  91.3 us (72%)
  Pallas kernels  17.9 us (14%)
  starting transfers between devices  10.8 us (9%)
  waiting for transfers between devices  5 us (4%)
    all_to_all x4, blocking collectives, exchange(): return lax.all_to_all(x, ALL, 0, 0, axis_index_groups=groups, tiled=True)  91.3 us
    pallas_call x1, Pallas kernels, finish(): pl.pallas_call(finish_kernel, in_specs=[pl.BlockSpec(memory_space=pltpu.S...  10.1 us
    ppermute x1, starting transfers between devices, body(): both = keep + lax.ppermute(send, ALL, PARTNERS)  8.75 us
    pallas_call x1, Pallas kernels, local_product(): pl.pallas_call(product_kernel, grid_spec=pltpu.PrefetchScalarGridSpec(num...  5.8 us
    ppermute x1, waiting for transfers between devices, body(): both = keep + lax.ppermute(send, ALL, PARTNERS)  3.76 us
  transfers between devices with their start and end apart: 2, of which 2 were waited for; matrix products, arithmetic and copies ran while one was open for 0% of the time, Pallas kernels for 0%

profile of v7, /device:TPU:1, one launch (start us, length us, event | category | flops | bytes accessed | tf_op | source)
XLA Modules:
  0.0 125.9 jit_solution(13430429287314955361)
XLA Ops:
  0.0 5.8 %local_product.1 = (f32[8,32,8,256]{3,2,1,0:T(8,128)S(1)}, f32[8,32,8,256]{3,2,1,0:T(8,128)S(1)}) custom-call(s32[7]{0:T(128)} %row_ref.1, s32[7]{0:T(128)} %col_ref.1, s32[1]{0:T(128)} %bitcast.2.core_ref, bf16[7,512,512]{2,1,0:T(8,128)(2,1)} %tile_ref.1, f32[1024,256]{1,0:T(8,128)} %basis_ref.1), custom_call_target="tpu_custom_call" | custom-call | tf_op jit(solution)/shard_map/local_product/pallas_call | solution.py:80
  5.8 8.7 %collective-permute-start = (f32[8,32,8,256]{3,2,1,0:T(8,128)S(1)}, f32[8,32,8,256]{3,2,1,0:T(8,128)S(1)}, u32[]{:S(2)}, u32[]{:S(2)}) collective-permute-start(f32[8,32,8,256]{3,2,1,0:T(8,128)S(1)} %get-tuple-element.8), channel_id=1, source_target_pairs={{0,8},{1,9},{2,10},{3,11},{4,12},{5,13},{6,14},{7,15},{8,0},{9,1},... | collective-permute-start | bytes 6291464 | tf_op jit(solution)/shard_map/ppermute | solution.py:271
  14.6 3.8 %collective-permute-done = f32[8,32,8,256]{3,2,1,0:T(8,128)S(1)} collective-permute-done((f32[8,32,8,256]{3,2,1,0:T(8,128)S(1)}, f32[8,32,8,256]{3,2,1,0:T(8,128)S(1)}, u32[]{:S(2)}, u32[]{:S(2)}) %collective-permute-start) | collective-permute-done | bytes 2097184 | tf_op jit(solution)/shard_map/ppermute | solution.py:271
  18.3 0.3 add.7
  18.6 28.9 %all_to_all.20 = f32[8,32,8,256]{3,2,1,0:T(8,128)S(1)} all-to-all(f32[8,32,8,256]{3,2,1,0:T(8,128)S(1)} %add.7), channel_id=1, replica_groups={{0,1,4,5,64,65,68,69},{2,3,6,7,66,67,70,71},{16,17,20,21,80,81,84,85},{..., dimensions={0} | all-to-all | bytes 4194304 | tf_op jit(solution)/shard_map/all_to_all | solution.py:260
  47.5 0.1 reduce_sum.18
  47.6 19.8 %all_to_all.21 = f32[32,8,256]{2,1,0:T(8,128)S(1)} all-to-all(f32[32,8,256]{2,1,0:T(8,128)S(1)} %reduce_sum.18), channel_id=1, replica_groups={{0,2,16,18,32,34,48,50,128,130,144,146,160,162,176,178,256,258,272,274,..., dimensions={0} | all-to-all | bytes 524288 | tf_op jit(solution)/shard_map/all_to_all | solution.py:260
  67.5 20.9 %all_to_all.22 = f32[32,8,256]{2,1,0:T(8,128)S(1)} all-to-all(f32[32,8,256]{2,1,0:T(8,128)S(1)} %broadcast_in_dim.6), channel_id=1, replica_groups={{0,2,16,18,32,34,48,50,128,130,144,146,160,162,176,178,256,258,272,274,..., dimensions={0} | all-to-all | bytes 524288 | tf_op jit(solution)/shard_map/all_to_all | solution.py:260
  88.4 0.2 broadcast_in_dim.7
  88.6 21.8 %all_to_all.23.rows_ref = f32[8,32,8,256]{3,2,1,0:T(8,128)S(1)} all-to-all(f32[8,32,8,256]{3,2,1,0:T(8,128)S(1)} %broadcast_in_dim.7), channel_id=1, replica_groups={{0,1,4,5,64,65,68,69},{2,3,6,7,66,67,70,71},{16,17,20,21,80,81,84,85},{..., dimensions={0} | all-to-all | bytes 4194304 | tf_op jit(solution)/shard_map/all_to_all | solution.py:260
  110.3 2.0 %gram_terms.1.gram_ref = f32[256,256]{1,0:T(8,128)S(1)} custom-call(f32[2048,256]{1,0:T(8,128)S(1)} %bitcast.4), custom_call_target="tpu_custom_call" | custom-call | tf_op jit(solution)/shard_map/gram_terms/pallas_call | solution.py:119
  112.3 2.1 %collective-permute-start.1 = (f32[256,256]{1,0:T(8,128)S(1)}, f32[256,256]{1,0:T(8,128)S(1)}, u32[]{:S(2)}, u32[]{:S(2)}) collective-permute-start(f32[256,256]{1,0:T(8,128)S(1)} %gram_terms.1.gram_ref), channel_id=1, source_target_pairs={{0,8},{1,9},{2,10},{3,11},{4,12},{5,13},{6,14},{7,15},{8,0},{9,1},... | collective-permute-start | bytes 786440 | tf_op jit(solution)/shard_map/ppermute | solution.py:276
  114.5 0.1 pad_add_fusion.at_ref
  114.5 1.2 collective-permute-done.1.other_ref
  115.8 10.1 %finish.1 = f32[64,256]{1,0:T(8,128)} custom-call(s32[2]{0:T(128)S(1)} %pad_add_fusion.at_ref, f32[256,256]{1,0:T(8,128)S(1)} %gram_terms.1.gram_ref, f32[256,256]{1,0:T(8,128)S(1)} %collective-permute-done.1.other_ref, f32[8,32,8,256]{3,2,1,0:T(8,128)S(1)} %all_to_all.23.rows_ref), custom_call_target="tpu_custom_call" | custom-call | tf_op jit(solution)/shard_map/finish/pallas_call | solution.py:228
  (2 shorter events, 0.1 us)
Async XLA Ops:
  5.8 12.5 %collective-permute-start = (f32[8,32,8,256]{3,2,1,0:T(8,128)S(1)}, f32[8,32,8,256]{3,2,1,0:T(8,128)S(1)}, u32[]{:S(2)}, u32[]{:S(2)}) collective-permute-start(f32[8,32,8,256]{3,2,1,0:T(8,128)S(1)} %get-tuple-element.8), channel_id=1, source_target_pairs={{0,8},{1,9},{2,10},{3,11},{4,12},{5,13},{6,14},{7,15},{8,0},{9,1},... | collective-permute-start | bytes 6291464 | tf_op jit(solution)/shard_map/ppermute | solution.py:271
  112.3 3.4 %collective-permute-start.1 = (f32[256,256]{1,0:T(8,128)S(1)}, f32[256,256]{1,0:T(8,128)S(1)}, u32[]{:S(2)}, u32[]{:S(2)}) collective-permute-start(f32[256,256]{1,0:T(8,128)S(1)} %gram_terms.1.gram_ref), channel_id=1, source_target_pairs={{0,8},{1,9},{2,10},{3,11},{4,12},{5,13},{6,14},{7,15},{8,0},{9,1},... | collective-permute-start | bytes 786440 | tf_op jit(solution)/shard_map/ppermute | solution.py:276
